TPU v7x, 256 devices: a whole 4x4x8 slice. The times are simulated.
256 devices in a mesh: wide: 64 (over y, z, core), narrow: 4 (over x).
Axes of the slice: x: 4, y: 4, z: 8, core: 2. Of those that a mesh axis runs over, the one named last changes fastest.
Arguments:
- residual_in: bfloat16 [128, 7168], P('wide', 'narrow'), may hold values from -2 to 2
- query_nope: bfloat16 [128, 64, 128], P('wide', 'narrow'), may hold values from -6 to 6
- query_rope: bfloat16 [128, 64, 64], P('wide', 'narrow'), may hold values from -8 to 8
- absorb_key: bfloat16 [64, 128, 512], P('narrow'), may hold values from -0.5 to 0.5
- absorb_value: bfloat16 [64, 512, 128], P('narrow'), may hold values from -0.25 to 0.25
- latent_cache: bfloat16 [128, 2048, 576], P('wide'), may hold values from -8 to 8
- cache_lengths: int32 [128], P('wide'), may hold values from 256 to 2048, as said below
- slot_rows: int32 [128], replicated, may hold values from 0 to 127, each once
- out_proj: bfloat16 [8192, 7168], P('wide', 'narrow'), may hold values from -0.0625 to 0.0625
- norm_gain: bfloat16 [7168], P('narrow'), may hold values from 0.25 to 1.75
- gate_weight: bfloat16 [7168, 18432], P('narrow', 'wide'), may hold values from -0.0625 to 0.0625
- up_weight: bfloat16 [7168, 18432], P('narrow', 'wide'), may hold values from -0.0625 to 0.0625
- down_weight: bfloat16 [18432, 7168], P('wide', 'narrow'), may hold values from -0.046875 to 0.046875
Outputs:
- residual_out: bfloat16 [128, 7168], P('wide', 'narrow')
Inputs may be any that keep to these rules, and one draw needn't show every extreme that they name: `cache_lengths`: every slot has at least 256 live positions; in every draw some slot is full. `slot_rows`: each batch row is named by exactly one slot.
All inputs are finite; a program needn't handle non-finite values.
Results may differ from a plain program's by a relative error of at most 0.009.
Values may be sent and summed in bfloat16 or wider, within the bound.
A program may use at most 64 MiB of HBM per device.

v0:
```python
import math

import jax
import jax.numpy as jnp
from jax import lax
from jax.sharding import PartitionSpec as P

D = 7168


def shards(
    residual_in,
    query_nope,
    query_rope,
    absorb_key,
    absorb_value,
    latent_cache,
    cache_lengths,
    slot_rows,
    out_proj,
    norm_gain,
    gate_weight,
    up_weight,
    down_weight,
):
    slot_count = latent_cache.shape[0]
    head_size = query_nope.shape[2]
    latent_width = absorb_key.shape[2]
    group_index = lax.axis_index("wide")
    packed_queries = jnp.concatenate([query_nope, query_rope], axis=2)
    gathered = lax.all_gather(packed_queries, "wide", axis=0, tiled=True)
    my_rows = lax.dynamic_slice_in_dim(slot_rows, group_index * slot_count, slot_count)
    selected = jnp.take(gathered, my_rows, axis=0)
    query_latent = jnp.einsum(
        "rhd,hdc->rhc", selected[:, :, :head_size], absorb_key, preferred_element_type=jnp.float32
    ).astype(jnp.bfloat16)
    full_query = jnp.concatenate([query_latent, selected[:, :, head_size:]], axis=2)
    scale = 1.0 / math.sqrt(full_query.shape[2] - latent_width + head_size)
    scores = (
        jnp.einsum("rhc,rtc->rht", full_query, latent_cache, preferred_element_type=jnp.float32)
        * scale
    )
    positions = jnp.arange(latent_cache.shape[1], dtype=jnp.int32)
    live = positions[None, None, :] < cache_lengths[:, None, None]
    scores = jnp.where(live, scores, -jnp.inf)
    highest = jnp.max(scores, axis=2, keepdims=True)
    weights = jnp.where(live, jnp.exp(scores - highest), 0.0)
    probs = (weights / jnp.sum(weights, axis=2, keepdims=True)).astype(jnp.bfloat16)
    context = jnp.einsum("rht,rtc->rhc", probs, latent_cache, preferred_element_type=jnp.float32)
    context = context[:, :, :latent_width].astype(jnp.bfloat16)
    heads_out = jnp.einsum(
        "rhc,hcd->rhd", context, absorb_value, preferred_element_type=jnp.float32
    ).astype(jnp.bfloat16)
    every_head = lax.all_gather(heads_out, "narrow", axis=1, tiled=True)
    flat_heads = every_head.reshape(slot_count, -1)
    head_columns = lax.all_to_all(flat_heads, "wide", split_axis=1, concat_axis=0, tiled=True)
    inverse = jnp.argsort(slot_rows)
    attention = lax.psum_scatter(
        jnp.dot(
            jnp.take(head_columns, inverse, axis=0), out_proj, preferred_element_type=jnp.float32
        ),
        "wide",
        scatter_dimension=0,
        tiled=True,
    )
    middle = residual_in.astype(jnp.float32) + attention
    square_sum = lax.psum(jnp.sum(middle * middle, axis=1), "narrow")
    normed = (
        middle * lax.rsqrt(square_sum / D + 1e-06)[:, None] * norm_gain.astype(jnp.float32)
    ).astype(jnp.bfloat16)
    hidden_cols = gate_weight.shape[1]
    row_piece = lax.all_gather(normed, "wide", axis=0, tiled=True)
    local_terms = jnp.concatenate(
        [
            jnp.dot(row_piece, gate_weight, preferred_element_type=jnp.float32),
            jnp.dot(row_piece, up_weight, preferred_element_type=jnp.float32),
        ],
        axis=1,
    )
    summed = lax.psum(local_terms, "narrow")
    hidden = (jax.nn.silu(summed[:, :hidden_cols]) * summed[:, hidden_cols:]).astype(jnp.bfloat16)
    ffn_total = lax.psum_scatter(
        jnp.dot(hidden, down_weight, preferred_element_type=jnp.float32),
        "wide",
        scatter_dimension=0,
        tiled=True,
    )
    return (middle + ffn_total).astype(jnp.bfloat16)


def solution(mesh):
    in_specs = (
        P("wide", "narrow"),
        P("wide", "narrow", None),
        P("wide", "narrow", None),
        P("narrow", None, None),
        P("narrow", None, None),
        P("wide", None, None),
        P("wide"),
        P(),
        P("wide", "narrow"),
        P("narrow"),
        P("narrow", "wide"),
        P("narrow", "wide"),
        P("wide", "narrow"),
    )
    out_specs = P("wide", "narrow")
    return jax.shard_map(shards, mesh=mesh, in_specs=in_specs, out_specs=out_specs, check_vma=False)
```

profile of v0, /device:TPU:1, one launch (start us, length us, event | category | flops | bytes accessed | tf_op | source)
XLA Modules:
  0.0 590.5 jit_solution(973563443931683544)
XLA Ops:
  6.5 0.0 copy-start
  6.5 0.9 compare_and_fusion
  7.4 0.7 pad_maximum_fusion.1
  8.2 55.1 %all_gather.9 = bf16[128,16,192]{2,1,0:T(8,128)(2,1)S(1)} all-gather(bf16[2,16,192]{2,1,0:T(8,128)(2,1)S(1)} %pad_maximum_fusion.1), channel_id=1, replica_groups=mesh['wide'=64,'narrow'=4] {'wide'}, dimensions={0}, use_global_device_ids=true | all-gather | bytes 798720 | tf_op jit(solution)/shard_map/all_gather | solution.py:31
  63.3 0.5 gather_fusion
  63.8 0.1 broadcast_select_fusion
  63.9 0.7 iota_compare_fusion
  64.6 0.0 copy-done
  64.6 0.4 fusion.21
  65.0 3.1 fusion.4
  68.2 0.2 fusion.29
  68.4 3.7 fusion.7
  72.1 0.0 copy-start.4
  72.1 0.0 copy-start.1
  72.1 0.0 copy-start.5
  72.1 0.0 copy-start.2
  72.1 0.0 copy-start.3
  72.2 2.0 fusion.5
  74.2 10.1 %all_gather.10 = bf16[2,64,128]{2,0,1:T(2,128)(2,1)} all-gather(bf16[2,16,128]{2,0,1:T(2,128)(2,1)S(1)} %fusion.5), channel_id=1, replica_groups=mesh['wide'=64,'narrow'=4] {'narrow'}, dimensions={1}, use_global_device_ids=true | all-gather | bytes 40960 | tf_op jit(solution)/shard_map/all_gather | solution.py:54
  84.3 9.3 %all-to-all-start = ((bf16[2,64,128]{2,0,1:T(2,128)(2,1)}), bf16[2,64,128]{2,0,1:T(2,128)(2,1)S(1)}, u32[]{:S(2)}, u32[]{:S(2)}) async-start(bf16[2,64,128]{2,0,1:T(2,128)(2,1)} %all_gather.10), calls=%async_computation | async-start | bytes 65536 | tf_op jit(solution)/shard_map/all_to_all | solution.py:56
  93.6 0.0 all-reduce.8.cloned.1.call-start
  93.7 0.0 copy-done.4
  93.7 2.5 sort.17
  96.3 6.7 %all-to-all-done = bf16[2,64,128]{2,0,1:T(2,128)(2,1)S(1)} async-done(((bf16[2,64,128]{2,0,1:T(2,128)(2,1)}), bf16[2,64,128]{2,0,1:T(2,128)(2,1)S(1)}, u32[]{:S(2)}, u32[]{:S(2)}) %all-to-all-start) | async-done | bytes 32800 | tf_op jit(solution)/shard_map/all_to_all | solution.py:56
  103.0 0.7 gather_fusion.1
  103.7 0.0 copy-done.1
  103.7 1.3 fusion.16
  105.0 0.0 all-reduce.8.cloned.1.call-update
  105.0 0.0 all-reduce.6.cloned.1.call-start
  105.1 0.0 copy-done.5
  105.1 0.6 dynamic-slice
  106.3 178.1 %all-reduce.8.cloned.1.call-done = f32[128,1792]{1,0:T(8,128)} async-done(((f32[128,1792]{1,0:T(8,128)}), f32[128,1792]{1,0:T(8,128)}) %all-reduce.8.cloned.1.call-update) | async-done | bytes 917520
  284.4 0.0 copy-done.2
  284.4 1.0 multiply_reduce_fusion
  285.3 0.0 copy-done.3
  285.3 8.4 %psum.14 = f32[2]{0:T(128)S(1)} all-reduce(f32[2]{0:T(128)S(1)} %multiply_reduce_fusion), channel_id=1, replica_groups=mesh['wide'=64,'narrow'=4] {'narrow'}, use_global_device_ids=true, to_apply=%region_5.6 | all-reduce | flops 2 | bytes 16 | tf_op jit(solution)/shard_map/psum | solution.py:67
  293.8 0.9 fusion.23
  294.7 53.2 %all-gather = bf16[64,2,1792]{2,1,0:T(2,128)(2,1)S(1)} all-gather(bf16[1,2,1792]{2,1,0:T(2,128)(2,1)S(1)} %fusion.23), channel_id=1, replica_groups=mesh['wide'=64,'narrow'=4] {'wide'}, dimensions={0}, use_global_device_ids=true | all-gather | bytes 465920 | tf_op jit(solution)/shard_map/all_gather | solution.py:72
  347.8 0.2 reshape.59
  348.0 1.6 fusion.31
  349.6 1.6 fusion.30
  351.3 0.7 pad_maximum_fusion
  352.0 0.0 all-reduce.6.cloned.1.call-update
  352.1 0.0 all-reduce.10.cloned.1.call-start
  352.1 39.3 %all-reduce.6.cloned.1.call-done = f32[128,576]{0,1:T(8,128)} async-done(((f32[128,576]{0,1:T(8,128)}), f32[128,576]{0,1:T(8,128)}) %all-reduce.6.cloned.1.call-update) | async-done | bytes 294928 | tf_op jit(solution)/shard_map/psum | solution.py:80
  391.4 2.8 fusion.9
  394.2 0.0 all-reduce.10.cloned.1.call-update
  394.2 188.3 %all-reduce.10.cloned.1.call-done = f32[128,1792]{1,0:T(8,128)} async-done(((f32[128,1792]{1,0:T(8,128)}), f32[128,1792]{1,0:T(8,128)}) %all-reduce.10.cloned.1.call-update) | async-done | bytes 917520
  582.5 1.5 fusion.20
  (11 shorter events, 0.1 us)
Async XLA Ops:
  6.5 58.1 %copy-start = (bf16[16,128,512]{2,1,0:T(8,128)(2,1)S(1)}, bf16[16,128,512]{2,1,0:T(8,128)(2,1)}, u32[]{:S(2)}) copy-start(bf16[16,128,512]{2,1,0:T(8,128)(2,1)} %param.16) | copy-start | bytes 6291460
  72.1 21.6 %copy-start.4 = (s32[128]{0:T(128)S(1)}, s32[128]{0:T(128)}, u32[]{:S(2)}) copy-start(s32[128]{0:T(128)} %param.20) | copy-start | bytes 1540
  72.1 31.6 %copy-start.1 = (bf16[128,1792]{1,0:T(8,128)(2,1)S(1)}, bf16[128,1792]{1,0:T(8,128)(2,1)}, u32[]{:S(2)}) copy-start(bf16[128,1792]{1,0:T(8,128)(2,1)} %param.21) | copy-start | bytes 1376260
  72.1 32.9 %copy-start.5 = (u32[256]{0:T(256)S(1)}, u32[256]{0:T(256)}, u32[]{:S(2)}) copy-start(u32[256]{0:T(256)} %constant.62) | copy-start | bytes 3076
  72.1 212.3 %copy-start.2 = (bf16[2,1792]{1,0:T(2,128)(2,1)S(1)}, bf16[2,1792]{1,0:T(2,128)(2,1)}, u32[]{:S(2)}) copy-start(bf16[2,1792]{1,0:T(2,128)(2,1)} %param.13) | copy-start | bytes 21508
  72.1 213.2 %copy-start.3 = (bf16[1792]{0:T(1024)(128)(2,1)S(1)}, bf16[1792]{0:T(1024)(128)(2,1)}, u32[]{:S(2)}) copy-start(bf16[1792]{0:T(1024)(128)(2,1)} %param.22) | copy-start | bytes 10756
  84.3 18.7 %all-to-all-start = ((bf16[2,64,128]{2,0,1:T(2,128)(2,1)}), bf16[2,64,128]{2,0,1:T(2,128)(2,1)S(1)}, u32[]{:S(2)}, u32[]{:S(2)}) async-start(bf16[2,64,128]{2,0,1:T(2,128)(2,1)} %all_gather.10), calls=%async_computation | async-start | bytes 65536 | tf_op jit(solution)/shard_map/all_to_all | solution.py:56
  93.6 190.7 %all-reduce.8.cloned.1.call-start = ((), (), s32[]{:S(2)}) async-start(), calls=%async_computation.2 | async-start | bytes 1835008
  105.0 286.4 %all-reduce.6.cloned.1.call-start = ((), (), s32[]{:S(2)}) async-start(), calls=%async_computation.1 | async-start | bytes 589824 | tf_op jit(solution)/shard_map/psum | solution.py:80
  352.1 230.4 %all-reduce.10.cloned.1.call-start = ((), (), s32[]{:S(2)}) async-start(), calls=%async_computation.3 | async-start | bytes 1835008
Sparse Core Ops, SparseCore 0:
  105.1 179.2 all-reduce.7
  352.2 39.1 all-reduce.5
  394.8 187.5 all-reduce.9
where the time goes:
time: 593 us; the launch traced here: 590 us
  waiting for transfers between devices  412 us (69%)
  blocking collectives  127 us (21%)
  matrix products  16.6 us (3%)
  between operations  13.9 us (2%)
  starting transfers between devices  9.47 us (2%)
  other arithmetic  9.27 us (2%)
    unnamed x5, waiting for transfers between devices  366 us
    all_gather x1, blocking collectives, shards(): gathered = lax.all_gather(packed_queries, 'wide', axis=0, tiled=True)  55.1 us
    all_gather x1, blocking collectives, shards(): row_piece = lax.all_gather(normed, 'wide', axis=0, tiled=True)  53.2 us
    psum x1, waiting for transfers between devices, shards(): summed = lax.psum(local_terms, 'narrow')  39.3 us
  transfers between devices with their start and end apart: 4, of which 4 were waited for; matrix products, arithmetic and copies ran while one was open for 1% of the time, Pallas kernels for 0%

commit v1 on v0

v1 whole, which is shorter than its diff:
```python
import math

import jax
import jax.numpy as jnp
from jax import lax
from jax.experimental import pallas as pl
from jax.experimental.pallas import tpu as pltpu
from jax.sharding import PartitionSpec as P

D = 7168
MESH = pl.DeviceIdType.MESH
F32 = jnp.float32
BF = jnp.bfloat16
COLS = 1792
SCALE = 1.0 / math.sqrt(192)
ANY = pl.BlockSpec(memory_space=pl.ANY)
SMEM = pl.BlockSpec(memory_space=pltpu.SMEM)
VM = pl.BlockSpec(memory_space=pltpu.VMEM)


def dot(a, b):
    return jnp.dot(a, b, preferred_element_type=F32)


def dot_nt(a, b):
    return lax.dot_general(a, b, (((1,), (1,)), ((), ())), preferred_element_type=F32)


def iota(shape, axis):
    return lax.broadcasted_iota(jnp.int32, shape, axis)


def swap_halves(tile):
    return jnp.concatenate([tile[:, 64:], tile[:, :64]], axis=1)


def kernel(
    slots, lengths, slot_vec, gain_v,
    res_h, qn_h, qr_h, ak_h, av_h, kv_h, wo_h, wg_h, wu_h, wd_h,
    out,
    res, qr, ak, av, kv, wo, wg, wu, wd, lsem,
    gq, sq, rq, a1s, a1r, a2s, a2r,
    c1b, c1r, c2f, c2b, hb, c1ss, c1rs, c2ss, c2rs,
    pm, gains, resmask,
    d0b, d0r, pown, d1b, d1r, att, asum, d2b, d2r, ss_d, rs_d,
    f1, f2, f3, ss_f, rs_f,
    g1b, g1r, hid, ss_g, rs_g,
    h0b, h0r, pown2, h1b, h1r, h2b, h2f, h2r, ss_h, rs_h,
):
    w = lax.axis_index("wide")
    x = lax.axis_index("narrow")
    y, z, c = w // 16, (w // 2) % 8, w % 2
    yc = y * 2 + c

    def wid(y_, z_, c_):
        return y_ * 16 + z_ * 2 + c_

    def rcopy(src, dst, ssem, rsem, w_, x_):
        return pltpu.make_async_remote_copy(
            src_ref=src, dst_ref=dst, send_sem=ssem, recv_sem=rsem,
            device_id=(w_, x_), device_id_type=MESH,
        )

    loads = []

    def load(src, dst):
        cp = pltpu.make_async_copy(src, dst, lsem.at[len(loads)])
        cp.start()
        loads.append(cp)
        return cp

    l_qn = load(qn_h, gq.at[yc, pl.ds(0, 2)])
    l_qr = load(qr_h, qr)
    l_ak = load(ak_h, ak)
    l_res = load(res_h, res)
    l_kv = load(kv_h, kv)
    l_av = load(av_h, av)
    l_wo = load(wo_h, wo)
    l_wg = load(wg_h, wg)
    l_wu = load(wu_h, wu)
    l_wd = load(wd_h, wd)

    bar = pltpu.get_barrier_semaphore()

    def greet(w_, x_):
        pl.semaphore_signal(bar, inc=1, device_id=(w_, x_), device_id_type=MESH)

    for k in range(1, 8):
        t = (yc + k) % 8
        greet(wid(t // 2, z, t % 2), x)
    for k in range(1, 8):
        greet(wid(y, (z + k) % 8, c), x)
    for k in range(1, 4):
        greet(w, (x + k) % 4)
    for ys in range(4):
        for cs in range(2):
            @pl.when(jnp.logical_or(x != y, jnp.logical_or(ys != y, cs != c)))
            def _():
                greet(wid(ys, z, cs), y)
    pl.semaphore_wait(bar, 25 - jnp.where(x == y, 1, 0))

    l_qr.wait()
    gq[yc, 2] = jnp.concatenate([qr[0], qr[1]], axis=1)
    l_qn.wait()
    sends = []
    cps = []
    for k in range(1, 8):
        t = (yc + k) % 8
        cp = rcopy(gq.at[yc], gq.at[yc], a1s.at[k - 1], a1r.at[k - 1], wid(t // 2, z, t % 2), x)
        cp.start()
        cps.append(cp)
    sends += cps

    sv = slot_vec[...]
    srow = (sv & 2) * 32 + (sv // 32) * 16 + ((sv // 4) & 7) * 2 + (sv & 1)
    rho = iota((128, 128), 0)
    own_first = jnp.where(rho < 64, rho + 64 * c, rho - 64 * c)
    hot = jnp.where(srow == own_first, 1.0, 0.0).astype(BF)
    sl = iota((128, 128), 0)
    sg = (sl // 32) * 32 + ((sl // 2) & 1) * 16 + ((sl // 4) & 7) * 2 + (sl & 1)
    arrange = jnp.where(sg == iota((128, 128), 1), 1.0, 0.0).astype(BF)
    pm[...] = dot(hot, arrange).astype(BF)
    l_res.wait()
    resf = res[...].astype(F32)
    spread = jnp.concatenate([resf] * 8, axis=0)
    resmask[...] = jnp.where(iota((16, COLS), 0) // 2 == z, spread, 0.0)
    gfull = gain_v[...].astype(F32)
    for j in range(7):
        gains[j] = gfull[:, 256 * j : 256 * j + 256]
    r32 = iota((32, 32), 0)
    c32 = iota((32, 32), 1)
    by_dest = jnp.where(c32 == (r32 & 1) * 16 + (r32 // 4) * 2 + ((r32 // 2) & 1), 1.0, 0.0).astype(BF)
    by_core = jnp.where(c32 == ((r32 // 2) & 7) * 4 + (r32 // 16) * 2 + (r32 & 1), 1.0, 0.0).astype(BF)

    for cp in cps:
        cp.wait_recv()

    low = iota((16, 128), 1) < 64
    for zp in range(8):
        ropes = []
        for s in range(2):
            r = slots[wid(y, zp, c) * 2 + s]
            i8 = (r // 32) * 2 + ((r // 2) & 1)
            i = r & 1
            sq[zp, s] = gq[i8, i]
            tile = gq[i8, 2].astype(F32)
            ropes.append(jnp.where(i == s, tile, swap_halves(tile)))
        sq[zp, 2] = jnp.where(low, ropes[0], ropes[1]).astype(BF)
    cps = []
    for k in range(1, 8):
        zt = (z + k) % 8
        cp = rcopy(sq.at[zt], rq.at[z], a2s.at[k - 1], a2r.at[k - 1], wid(y, zt, c), x)
        cp.start()
        cps.append(cp)
    sends += cps
    rq[z] = sq[z]
    l_ak.wait()
    l_kv.wait()
    for cp in cps:
        cp.wait_recv()

    q_parts, ropes = [], []
    for s in range(2):
        r = slots[w * 2 + s]
        zr = (r // 4) & 7
        q_parts.append(rq[zr, s])
        ropes.append(rq[zr, 2][:, 64 * s : 64 * s + 64])
    qn = jnp.concatenate(q_parts, axis=0)
    wide_q = jnp.concatenate([qn] * 16, axis=1)
    own_head = iota((32, 2048), 1) // 128 == (iota((32, 2048), 0) & 15)
    wide_q = jnp.where(own_head, wide_q, jnp.zeros_like(wide_q))
    qlat = dot(wide_q, ak[...].reshape(2048, 512)).astype(BF)
    ctxs = []
    for s in range(2):
        sc = dot_nt(qlat[16 * s : 16 * s + 16], kv[s, :, 0:512])
        sc = (sc + dot_nt(ropes[s], kv[s, :, 512:576])) * SCALE
        live = iota((16, 2048), 1) < lengths[s]
        sc = jnp.where(live, sc, -1e30)
        e = jnp.exp(sc - jnp.max(sc, axis=1, keepdims=True))
        e = jnp.where(live, e, 0.0)
        p = (e / jnp.sum(e, axis=1, keepdims=True)).astype(BF)
        ctxs.append(dot(p, kv[s, :, 0:512]).astype(BF))
    ctx = jnp.concatenate(ctxs, axis=0)
    wide_c = jnp.concatenate([ctx] * 16, axis=1)
    own_head = iota((32, 8192), 1) // 512 == (iota((32, 8192), 0) & 15)
    wide_c = jnp.where(own_head, wide_c, jnp.zeros_like(wide_c))
    l_av.wait()
    heads = dot(wide_c, av[...].reshape(8192, 128)).astype(BF)

    hp = dot(by_dest, heads)
    for zp in range(8):
        c1b[zp] = hp[4 * zp : 4 * zp + 4]
    cps = []
    for k in range(1, 8):
        zt = (z + k) % 8
        cp = rcopy(c1b.at[zt], c1r.at[z], c1ss.at[k - 1], c1rs.at[k - 1], wid(y, zt, c), x)
        cp.start()
        cps.append(cp)
    sends += cps
    c1r[z] = c1b[z]
    for cp in cps:
        cp.wait_recv()
    for zs in range(8):
        c2f[4 * zs : 4 * zs + 4] = c1r[zs]
    both = dot(by_core, c2f[...].astype(BF)).astype(BF)
    c2b[0] = both[0:16]
    c2b[1] = both[16:32]
    off_self = []
    for xt in range(4):
        for ct in range(2):
            other = jnp.logical_or(x != y, jnp.logical_or(xt != x, ct != c))
            cp = rcopy(
                c2b.at[ct], hb.at[yc], c2ss.at[xt * 2 + ct], c2rs.at[yc], wid(x, z, ct), xt
            )

            @pl.when(other)
            def _():
                cp.start()

            off_self.append((other, cp))

    @pl.when(x == y)
    def _():
        hb[yc] = c2b[c]

    l_wo.wait()
    for ys in range(4):
        for cs in range(2):
            j = ys * 2 + cs

            @pl.when(jnp.logical_or(x != y, j != yc))
            def _():
                rcopy(c2b.at[0], hb.at[j], c2ss.at[j], c2rs.at[j], wid(ys, z, cs), y).wait_recv()

    heads_all = dot(pm[...], hb[...].reshape(128, 128)).astype(BF)

    def to_core(terms, send_buf, recv_buf, own_buf, ssem, rsem):
        send_buf[...] = terms(64).astype(BF).reshape(4, 16, COLS)
        cp = rcopy(send_buf, recv_buf, ssem.at[0], rsem.at[0], wid(y, z, 1 - c), x)
        cp.start()
        own_buf[...] = terms(0).reshape(4, 16, COLS)
        cp.wait_recv()
        return cp

    def along_y(own_buf, recv_core, send_buf, recv_buf, ssem, rsem):
        for yp in range(4):
            total = own_buf[yp] + recv_core[yp].astype(F32)
            own_buf[yp] = total
            send_buf[yp] = total.astype(BF)
        cps = []
        for k in range(1, 4):
            yt = (y + k) % 4
            cp = rcopy(send_buf.at[yt], recv_buf.at[k - 1], ssem.at[k], rsem.at[k], wid(yt, z, c), x)
            cp.start()
            cps.append(cp)
        total = own_buf[y]
        for k in range(3):
            cps[k].wait_recv()
            total = total + recv_buf[k].astype(F32)
        return total, cps

    sends.append(
        to_core(lambda o: dot(heads_all[o : o + 64], wo[...]), d0b, d0r, pown, ss_d, rs_d)
    )
    total, cps = along_y(pown, d0r, d1b, d1r, ss_d, rs_d)
    sends += cps
    att[...] = total
    total = total + resmask[...]
    for j in range(7):
        piece = total[:, 256 * j : 256 * j + 256]
        asum[j] = piece
        d2b[j] = piece.astype(BF)
    guarded = []
    for k in range(1, 8):
        zt = (z + k) % 8
        cp = rcopy(
            d2b.at[lax.min(zt, 6)], d2r.at[k - 1], ss_d.at[3 + k], rs_d.at[3 + k], wid(y, zt, c), x
        )

        @pl.when(zt < 7)
        def _():
            cp.start()

        guarded.append((zt < 7, cp))

    zc = lax.min(z, 6)

    def f1_copy(k):
        zt = (z + k) % 8
        return rcopy(
            f1.at[zc], f1.at[zc], ss_f.at[k - 1], rs_f.at[k - 1], wid(y, zt, c), x
        )

    @pl.when(z < 7)
    def _():
        mid = asum[zc]
        for k in range(1, 8):
            guarded[k - 1][1].wait_recv()
            mid = mid + d2r[k - 1].astype(F32)
        f1[zc] = (mid * gains[zc]).astype(BF)
        for k in range(1, 8):
            f1_copy(k).start()

    for k in range(1, 8):
        @pl.when((z + 8 - k) % 8 < 7)
        def _():
            f1_copy(k).wait_recv()

    x16 = jnp.concatenate([f1[j] for j in range(7)], axis=1)
    f2[y, :, 0:COLS] = x16
    plain = x16.astype(F32) / gfull
    sums = jnp.sum(plain * plain, axis=1, keepdims=True)
    high = sums.astype(BF).astype(F32)
    rest = sums - high
    f2[y, :, COLS : COLS + 128] = jnp.where(iota((16, 128), 1) < 64, high, rest).astype(BF)
    ycps, ccps = [], []
    for k in range(1, 4):
        yt = (y + k) % 4
        cp = rcopy(f2.at[y], f2.at[y], ss_f.at[6 + k], rs_f.at[6 + k], wid(yt, z, c), x)
        cp.start()
        ycps.append(cp)

    def across(k):
        yb = (y + 4 - k) % 4
        cp = rcopy(f2.at[yb], f3.at[yb], ss_f.at[10 + k], rs_f.at[10 + k], wid(y, z, 1 - c), x)
        cp.start()
        ccps.append(cp)

    across(0)
    for k in range(1, 4):
        ycps[k - 1].wait_recv()
        across(k)
    sends += ycps + ccps

    l_wg.wait()
    l_wu.wait()

    def gate_up(rows, first):
        data = rows[...].reshape(64, COLS + 128)
        act = data[:, 0:COLS]
        tag = data[:, COLS:]
        gate = dot(act, wg[...]).astype(BF)
        up = dot(act, wu[...]).astype(BF)
        for b in range(2):
            g1b[first + b, :, 256:384] = tag[32 * b : 32 * b + 32]
            g1b[first + b, :, 640:768] = tag[32 * b : 32 * b + 32]
            g1b[first + b, :, 0:288] = gate[32 * b : 32 * b + 32]
            g1b[first + b, :, 384:672] = up[32 * b : 32 * b + 32]

    gate_up(f2, 0)
    for cp in ccps:
        cp.wait_recv()
    gate_up(f3, 2)
    cps = []
    for k in range(1, 4):
        xt = (x + k) % 4
        cp = rcopy(g1b.at[xt], g1r.at[k - 1], ss_g.at[k - 1], rs_g.at[k - 1], w, xt)
        cp.start()
        cps.append(cp)
    sends += cps
    total = g1b[x].astype(F32)
    for k in range(3):
        cps[k].wait_recv()
        total = total + g1r[k].astype(F32)
    square = total[:, 288:289] + total[:, 320:321]
    norm = lax.rsqrt(square / D + 1e-06)
    gate = total[:, 0:288] * norm
    up = total[:, 384:672] * norm
    hid[x] = (gate / (1.0 + jnp.exp(-gate)) * up).astype(BF)
    cps = []
    for k in range(1, 4):
        xt = (x + k) % 4
        cp = rcopy(hid.at[x], hid.at[x], ss_g.at[2 + k], rs_g.at[2 + k], w, xt)
        cp.start()
        cps.append(cp)
    sends += cps
    l_wd.wait()
    for cp in cps:
        cp.wait_recv()

    hidden = hid[...].reshape(128, 288)
    sends.append(
        to_core(lambda o: dot(hidden[o : o + 64], wd[...]), h0b, h0r, pown2, ss_h, rs_h)
    )
    total, cps = along_y(pown2, h0r, h1b, h1r, ss_h, rs_h)
    sends += cps
    total = total + att[...]
    for zp in range(8):
        piece = total[2 * zp : 2 * zp + 2]
        h2f[zp] = piece
        h2b[zp] = piece.astype(BF)
    cps = []
    for k in range(1, 8):
        zt = (z + k) % 8
        cp = rcopy(h2b.at[zt], h2r.at[k - 1], ss_h.at[3 + k], rs_h.at[3 + k], wid(y, zt, c), x)
        cp.start()
        cps.append(cp)
    sends += cps
    total = res[...].astype(F32) + h2f[z]
    for k in range(7):
        cps[k].wait_recv()
        total = total + h2r[k].astype(F32)
    out[...] = total.astype(BF)

    for cp in sends:
        cp.wait_send()
    for cond, cp in off_self + guarded:
        @pl.when(cond)
        def _():
            cp.wait_send()

    @pl.when(z < 7)
    def _():
        for k in range(1, 8):
            f1_copy(k).wait_send()


def shards(
    residual_in, query_nope, query_rope, absorb_key, absorb_value, latent_cache, cache_lengths,
    slot_rows, out_proj, norm_gain, gate_weight, up_weight, down_weight,
):
    v = pltpu.VMEM
    sem = pltpu.SemaphoreType.DMA
    scratch = [
        v((2, COLS), BF), v((2, 16, 64), BF), v((16, 128, 512), BF), v((16, 512, 128), BF),
        v((2, 2048, 576), BF), v((128, COLS), BF), v((COLS, 288), BF), v((COLS, 288), BF),
        v((288, COLS), BF), sem((10,)),
        v((8, 3, 16, 128), BF), v((8, 3, 16, 128), BF), v((8, 3, 16, 128), BF),
        sem((7,)), sem((7,)), sem((7,)), sem((7,)),
        v((8, 4, 128), F32), v((8, 4, 128), F32), v((32, 128), F32), v((2, 16, 128), BF),
        v((8, 16, 128), BF), sem((7,)), sem((7,)), sem((8,)), sem((8,)),
        v((128, 128), BF), v((7, 1, 256), F32), v((16, COLS), F32),
        v((4, 16, COLS), BF), v((4, 16, COLS), BF), v((4, 16, COLS), F32), v((4, 16, COLS), BF),
        v((3, 16, COLS), BF), v((16, COLS), F32), v((7, 16, 256), F32), v((7, 16, 256), BF),
        v((7, 16, 256), BF), sem((11,)), sem((11,)),
        v((7, 16, 256), BF), v((4, 16, COLS + 128), BF), v((4, 16, COLS + 128), BF),
        sem((14,)), sem((14,)),
        v((4, 32, 768), BF), v((3, 32, 768), BF), v((4, 32, 288), BF), sem((6,)), sem((6,)),
        v((4, 16, COLS), BF), v((4, 16, COLS), BF), v((4, 16, COLS), F32), v((4, 16, COLS), BF),
        v((3, 16, COLS), BF), v((8, 2, COLS), BF), v((8, 2, COLS), F32), v((7, 2, COLS), BF),
        sem((11,)), sem((11,)),
    ]
    return pl.pallas_call(
        kernel,
        out_shape=jax.ShapeDtypeStruct((2, COLS), BF),
        in_specs=[SMEM, SMEM, VM, VM] + [ANY] * 10,
        out_specs=VM,
        scratch_shapes=scratch,
        compiler_params=pltpu.CompilerParams(
            collective_id=0, has_side_effects=True, vmem_limit_bytes=48 * 1024 * 1024
        ),
    )(
        slot_rows, cache_lengths, slot_rows.reshape(1, 128), norm_gain.reshape(1, COLS),
        residual_in, query_nope, query_rope, absorb_key, absorb_value, latent_cache, out_proj,
        gate_weight, up_weight, down_weight,
    )


def solution(mesh):
    in_specs = (
        P("wide", "narrow"),
        P("wide", "narrow", None),
        P("wide", "narrow", None),
        P("narrow", None, None),
        P("narrow", None, None),
        P("wide", None, None),
        P("wide"),
        P(),
        P("wide", "narrow"),
        P("narrow"),
        P("narrow", "wide"),
        P("narrow", "wide"),
        P("wide", "narrow"),
    )
    out_specs = P("wide", "narrow")
    return jax.shard_map(shards, mesh=mesh, in_specs=in_specs, out_specs=out_specs, check_vma=False)
```

time: 593 us -> 91.9 us (0.15)
  waiting for transfers between devices: 412 us -> 0 us
  blocking collectives: 127 us -> 0 us
  Pallas kernels: 0 us -> 77.7 us
  matrix products: 16.6 us -> 0 us
  between operations: 13.9 us -> 0.11 us
  local copies, waits for them, and re-layouts: 2.08 us -> 13.8 us
  starting transfers between devices: 9.47 us -> 0 us
  other arithmetic: 9.27 us -> 0 us
    unnamed x5 -> x0, waiting for transfers between devices: 366 us -> none
    all_gather x3 -> x0, blocking collectives: 118 us -> none  [the longest x1 55.1 us: shards(): gathered = lax.all_gather(packed_queries, 'wide', axis=0, tiled=True)]
    pallas_call x0 -> x1, Pallas kernels: none -> 77.7 us  [shards(): pl.pallas_call(kernel, out_shape=jax.ShapeDtypeStruct((2, COLS), BF), in_...]
    psum x1 -> x0, waiting for transfers between devices: 39.3 us -> none  [shards(): summed = lax.psum(local_terms, 'narrow')]
    dot_general x8 -> x0, matrix products: 16.6 us -> none  [the longest x1 3.71 us: shards(): jnp.einsum('rht,rtc->rhc', probs, latent_cache, preferred_element_type=jn...]
    unnamed x14 -> x18, local copies, waits for them, and re-layouts: 0.79 us -> 13.1 us
    all_to_all x1 -> x0, starting transfers between devices: 9.34 us -> none  [shards(): lax.all_to_all(flat_heads, 'wide', split_axis=1, concat_axis=0, tiled=True)]
    psum x1 -> x0, blocking collectives: 8.41 us -> none  [shards(): square_sum = lax.psum(jnp.sum(middle * middle, axis=1), 'narrow')]
  transfers between devices with their start and end apart: 4 -> 0, of which waited for: 4 -> 0; matrix products, arithmetic and copies ran while one was open for 1% -> 0% of each run, Pallas kernels for 0% -> 0%
where the time goes in v1:
time: 91.9 us; the launch traced here: 91.6 us
  Pallas kernels  77.7 us (85%)
  local copies, waits for them, and re-layouts  13.8 us (15%)
    pallas_call x1, Pallas kernels, shards(): pl.pallas_call(kernel, out_shape=jax.ShapeDtypeStruct((2, COLS), BF), in_...  77.7 us
    unnamed x18, local copies, waits for them, and re-layouts  13.1 us

profile of v1, /device:TPU:1, one launch (start us, length us, event | category | flops | bytes accessed | tf_op | source)
XLA Modules:
  0.0 91.6 jit_solution(16068953050243003274)
XLA Ops:
  0.0 0.7 reshape.7.gain_v
  0.7 1.8 %copy.15.wg_h = bf16[1792,288]{1,0:T(8,128)(2,1)S(1)} copy(bf16[1792,288]{0,1:T(8,128)(2,1)} %param.23) | data formatting | bytes 2064384 | tf_op args[10]
  2.5 1.8 %copy.16.wu_h = bf16[1792,288]{1,0:T(8,128)(2,1)S(1)} copy(bf16[1792,288]{0,1:T(8,128)(2,1)} %param.24) | data formatting | bytes 2064384 | tf_op args[11]
  4.2 0.0 copy-start.1
  4.2 0.0 copy-start.2
  4.3 0.0 copy-start.3
  4.3 0.0 copy-start.4
  4.3 0.0 copy-start.5
  4.3 0.0 copy-start.6
  4.3 7.7 %copy.14.kv_h = bf16[2,2048,576]{2,1,0:T(8,128)(2,1)} copy(bf16[2,2048,576]{1,2,0:T(8,128)(2,1)} %param.18) | data formatting | bytes 9437184 | tf_op args[5]
  12.0 0.0 copy-done.1
  12.0 0.0 copy-done.2
  12.1 0.0 copy-done.3
  12.1 0.0 copy-done.4
  12.1 0.0 copy-done.5
  12.1 0.0 copy-done.6
  12.1 0.0 copy-start
  12.1 1.2 %copy-done = bf16[288,1792]{1,0:T(8,128)(2,1)S(1)} copy-done((bf16[288,1792]{1,0:T(8,128)(2,1)S(1)}, bf16[288,1792]{1,0:T(8,128)(2,1)}, u32[]{:S(2)}) %copy-start) | copy-done | bytes 1032216
  13.3 77.7 %shard_map.127 = bf16[2,1792]{1,0:T(2,128)(2,1)S(1)} custom-call(s32[128]{0:T(128)S(1)} %copy-done.5, s32[2]{0:T(128)S(1)} %copy-done.6, s32[1,128]{1,0:T(1,128)S(1)} %bitcast.1, bf16[1,1792]{1,0:T(2,128)(2,1)S(1)} %reshape.7.gain_v, bf16[2,1792]{1,0:T(2,128)(2,1)S(1)} %copy-done.4, bf16[2,16,128]{2,1,0:T(8,128)(2,1)S(1)} %copy-done.2, ...), custom_call_target="tpu_custom_call" | custom-call | tf_op jit(solution)/shard_map/pallas_call | solution.py:443
  91.0 0.6 copy.18
Async XLA Ops:
  4.2 7.8 %copy-start.1 = (bf16[128,1792]{1,0:T(8,128)(2,1)S(1)}, bf16[128,1792]{1,0:T(8,128)(2,1)}, u32[]{:S(2)}) copy-start(bf16[128,1792]{1,0:T(8,128)(2,1)} %wo_h.1) | copy-start | bytes 1376260
  4.2 7.8 %copy-start.2 = (bf16[2,16,128]{2,1,0:T(8,128)(2,1)S(1)}, bf16[2,16,128]{2,1,0:T(8,128)(2,1)}, u32[]{:S(2)}) copy-start(bf16[2,16,128]{2,1,0:T(8,128)(2,1)} %qn_h.1) | copy-start | bytes 24580
  4.3 7.8 %copy-start.3 = (bf16[2,16,64]{2,1,0:T(8,128)(2,1)S(1)}, bf16[2,16,64]{2,1,0:T(8,128)(2,1)}, u32[]{:S(2)}) copy-start(bf16[2,16,64]{2,1,0:T(8,128)(2,1)} %qr_h.1) | copy-start | bytes 12292
  4.3 7.8 %copy-start.4 = (bf16[2,1792]{1,0:T(2,128)(2,1)S(1)}, bf16[2,1792]{1,0:T(2,128)(2,1)}, u32[]{:S(2)}) copy-start(bf16[2,1792]{1,0:T(2,128)(2,1)} %res_h.1) | copy-start | bytes 21508
  4.3 7.8 %copy-start.5 = (s32[128]{0:T(128)S(1)}, s32[128]{0:T(128)}, u32[]{:S(2)}) copy-start(s32[128]{0:T(128)} %slots.1) | copy-start | bytes 1540
  4.3 7.8 %copy-start.6 = (s32[2]{0:T(128)S(1)}, s32[2]{0:T(128)}, u32[]{:S(2)}) copy-start(s32[2]{0:T(128)} %lengths.1) | copy-start | bytes 28
  12.1 1.2 %copy-start = (bf16[288,1792]{1,0:T(8,128)(2,1)S(1)}, bf16[288,1792]{1,0:T(8,128)(2,1)}, u32[]{:S(2)}) copy-start(bf16[288,1792]{1,0:T(8,128)(2,1)} %wd_h.1) | copy-start | bytes 3096580

commit v2 on v1

v2 whole, which is shorter than its diff:
```python
import math

import jax
import jax.numpy as jnp
from jax import lax
from jax.experimental import pallas as pl
from jax.experimental.pallas import tpu as pltpu
from jax.sharding import PartitionSpec as P

D = 7168
MESH = pl.DeviceIdType.MESH
F32 = jnp.float32
BF = jnp.bfloat16
COLS = 1792
GROUPS = ((0, 2), (2, 4), (4, 7))
NG = len(GROUPS)
FAR_FIRST = (4, 3, 5, 2, 6, 1, 7)
SCALE = 1.0 / math.sqrt(192)
HBM = pl.BlockSpec(memory_space=pltpu.HBM)
SMEM = pl.BlockSpec(memory_space=pltpu.SMEM)
VM = pl.BlockSpec(memory_space=pltpu.VMEM)


def dot(a, b):
    return jnp.dot(a, b, preferred_element_type=F32)


def dot_nt(a, b):
    return lax.dot_general(a, b, (((1,), (1,)), ((), ())), preferred_element_type=F32)


def iota(shape, axis):
    return lax.broadcasted_iota(jnp.int32, shape, axis)


def swap_halves(tile):
    return jnp.concatenate([tile[:, 64:], tile[:, :64]], axis=1)


def kernel(
    slots, lengths, slot_vec_h, gain_h,
    res_h, qn_h, qr_h, ak_h, av_h, kv_h, wo_h, wg_h, wu_h, wd_h,
    out,
    slot_vec, gain_v, res, qr, ak, av, kv, wo, wg, wu, wd, lsem,
    gq, sq, rq, a1s, a1r, a2s, a2r,
    c1b, c1r, c2f, c2b, hb, c1ss, c1rs, c2ss, c2rs,
    pm, gains, gain_inv, resmask,
    d0b, d0r, pown, d1b, d1r, att, ss_d, rs_d, asum, d2b, d2r, ss_z, rs_z,
    f1, f2, f3, ss_f1, rs_f1, ss_f2, rs_f2, ss_f3, rs_f3,
    g1b, g1r, hid, ss_g, rs_g, ss_x, rs_x,
    h0b, h0r, pown2, h1b, h1r, ss_h, rs_h, h2b, h2f, h2r, ss_o, rs_o,
):
    w = lax.axis_index("wide")
    x = lax.axis_index("narrow")
    y, z, c = w // 16, (w // 2) % 8, w % 2
    yc = y * 2 + c

    def wid(y_, z_, c_):
        return y_ * 16 + z_ * 2 + c_

    def rcopy(src, dst, ssem, rsem, w_, x_):
        return pltpu.make_async_remote_copy(
            src_ref=src, dst_ref=dst, send_sem=ssem, recv_sem=rsem,
            device_id=(w_, x_), device_id_type=MESH,
        )

    loads, held, sends = [], [], []

    def load(src, dst):
        cp = pltpu.make_async_copy(src, dst, lsem.at[len(loads)])
        cp.start()
        loads.append(cp)
        held.append(cp)
        return cp

    def need(cp):
        held[:] = [h for h in held if h is not cp]
        cp.wait()

    def finish():
        for cp in held:
            cp.wait()
        for cond, cp in sends:
            if cond is None:
                cp.wait_send()
            else:
                @pl.when(cond)
                def _():
                    cp.wait_send()

    def send(cp, cond=None):
        sends.append((cond, cp))
        if cond is None:
            cp.start()
        else:
            @pl.when(cond)
            def _():
                cp.start()
        return cp

    bar = pltpu.get_barrier_semaphore()

    def greet(w_, x_):
        pl.semaphore_signal(bar, inc=1, device_id=(w_, x_), device_id_type=MESH)

    for k in range(1, 8):
        t = (yc + k) % 8
        greet(wid(t // 2, z, t % 2), x)
    for k in range(1, 8):
        greet(wid(y, (z + k) % 8, c), x)
    for k in range(1, 4):
        greet(w, (x + k) % 4)
    for ys in range(4):
        for cs in range(2):
            @pl.when(jnp.logical_or(x != y, jnp.logical_or(ys != y, cs != c)))
            def _():
                greet(wid(ys, z, cs), y)
    l_qn = load(qn_h, gq.at[yc, pl.ds(0, 2)])
    l_qr = load(qr_h, qr)
    l_ak = load(ak_h, ak)
    l_sv = load(slot_vec_h, slot_vec)
    l_gain = load(gain_h, gain_v)
    l_res = load(res_h, res)
    l_kv = load(kv_h, kv)
    l_av = load(av_h, av)
    l_wo = load(wo_h, wo)
    l_wg = load(wg_h, wg)
    l_wu = load(wu_h, wu)
    l_wd = load(wd_h, wd)

    pl.semaphore_wait(bar, 25 - jnp.where(x == y, 1, 0))

    need(l_qr)
    gq[yc, 2] = jnp.concatenate([qr[0], qr[1]], axis=1)
    need(l_qn)
    cps = []
    for k in (4, 5, 2, 3, 6, 7, 1):
        t = (yc + k) % 8
        cp = rcopy(gq.at[yc], gq.at[yc], a1s.at[k - 1], a1r.at[k - 1], wid(t // 2, z, t % 2), x)
        cps.append(send(cp))

    need(l_sv)
    sv = slot_vec[...]
    srow = (sv & 2) * 32 + (sv // 32) * 16 + ((sv // 4) & 7) * 2 + (sv & 1)
    rho = iota((128, 128), 0)
    own_first = jnp.where(rho < 64, rho + 64 * c, rho - 64 * c)
    hot = jnp.where(srow == own_first, 1.0, 0.0).astype(BF)
    sl = iota((128, 128), 0)
    sg = (sl // 32) * 32 + ((sl // 2) & 1) * 16 + ((sl // 4) & 7) * 2 + (sl & 1)
    arrange = jnp.where(sg == iota((128, 128), 1), 1.0, 0.0).astype(BF)
    pm[...] = dot(hot, arrange).astype(BF)
    need(l_res)
    resf = res[...].astype(F32)
    spread = jnp.concatenate([resf] * 8, axis=0)
    resmask[...] = jnp.where(iota((16, COLS), 0) // 2 == z, spread, 0.0)
    need(l_gain)
    gfull = gain_v[...].astype(F32).reshape(1, COLS)
    for j in range(7):
        gains[j] = gfull[:, 256 * j : 256 * j + 256]
    gain_inv[...] = 1.0 / gfull
    r32 = iota((32, 32), 0)
    c32 = iota((32, 32), 1)
    by_dest = jnp.where(c32 == (r32 & 1) * 16 + (r32 // 4) * 2 + ((r32 // 2) & 1), 1.0, 0.0).astype(BF)
    by_core = jnp.where(c32 == ((r32 // 2) & 7) * 4 + (r32 // 16) * 2 + (r32 & 1), 1.0, 0.0).astype(BF)

    for cp in cps:
        cp.wait_recv()

    low = iota((16, 128), 1) < 64
    for zp in range(8):
        ropes = []
        for s in range(2):
            r = slots[wid(y, zp, c) * 2 + s]
            i8 = (r // 32) * 2 + ((r // 2) & 1)
            i = r & 1
            sq[zp, s] = gq[i8, i]
            tile = gq[i8, 2].astype(F32)
            ropes.append(jnp.where(i == s, tile, swap_halves(tile)))
        sq[zp, 2] = jnp.where(low, ropes[0], ropes[1]).astype(BF)
    cps = []
    for k in FAR_FIRST:
        zt = (z + k) % 8
        cp = rcopy(sq.at[zt], rq.at[z], a2s.at[k - 1], a2r.at[k - 1], wid(y, zt, c), x)
        cps.append(send(cp))
    rq[z] = sq[z]
    need(l_ak)
    need(l_kv)
    for cp in cps:
        cp.wait_recv()

    q_parts, ropes = [], []
    for s in range(2):
        r = slots[w * 2 + s]
        zr = (r // 4) & 7
        q_parts.append(rq[zr, s])
        ropes.append(rq[zr, 2][:, 64 * s : 64 * s + 64])
    qn = jnp.concatenate(q_parts, axis=0)
    wide_q = jnp.concatenate([qn] * 16, axis=1)
    own_head = iota((32, 2048), 1) // 128 == (iota((32, 2048), 0) & 15)
    wide_q = jnp.where(own_head, wide_q, jnp.zeros_like(wide_q))
    qlat = dot(wide_q, ak[...].reshape(2048, 512)).astype(BF)
    ctxs = []
    for s in range(2):
        sc = dot(qlat[16 * s : 16 * s + 16], kv[s, 0:512])
        sc = (sc + dot(ropes[s], kv[s, 512:576])) * SCALE
        live = iota((16, 2048), 1) < lengths[s]
        sc = jnp.where(live, sc, -1e30)
        e = jnp.exp(sc - jnp.max(sc, axis=1, keepdims=True))
        e = jnp.where(live, e, 0.0)
        p = (e / jnp.sum(e, axis=1, keepdims=True)).astype(BF)
        ctxs.append(dot_nt(p, kv[s, 0:512]).astype(BF))
    ctx = jnp.concatenate(ctxs, axis=0)
    wide_c = jnp.concatenate([ctx] * 16, axis=1)
    own_head = iota((32, 8192), 1) // 512 == (iota((32, 8192), 0) & 15)
    wide_c = jnp.where(own_head, wide_c, jnp.zeros_like(wide_c))
    need(l_av)
    heads = dot(wide_c, av[...].reshape(8192, 128)).astype(BF)

    hp = dot(by_dest, heads)
    for zp in range(8):
        c1b[zp] = hp[4 * zp : 4 * zp + 4]
    cps = []
    for k in FAR_FIRST:
        zt = (z + k) % 8
        cp = rcopy(c1b.at[zt], c1r.at[z], c1ss.at[k - 1], c1rs.at[k - 1], wid(y, zt, c), x)
        cps.append(send(cp))
    c1r[z] = c1b[z]
    for cp in cps:
        cp.wait_recv()
    for zs in range(8):
        c2f[4 * zs : 4 * zs + 4] = c1r[zs]
    both = dot(by_core, c2f[...].astype(BF)).astype(BF)
    c2b[0] = both[0:16]
    c2b[1] = both[16:32]
    for xt in range(4):
        for ct in range(2):
            other = jnp.logical_or(x != y, jnp.logical_or(xt != x, ct != c))
            cp = rcopy(
                c2b.at[ct], hb.at[yc], c2ss.at[xt * 2 + ct], c2rs.at[yc], wid(x, z, ct), xt
            )

            send(cp, other)

    @pl.when(x == y)
    def _():
        hb[yc] = c2b[c]

    need(l_wo)
    for ys in range(4):
        for cs in range(2):
            j = ys * 2 + cs

            @pl.when(jnp.logical_or(x != y, j != yc))
            def _():
                rcopy(c2b.at[0], hb.at[j], c2ss.at[j], c2rs.at[j], wid(ys, z, cs), y).wait_recv()

    heads_all = dot(pm[...], hb[...].reshape(128, 128)).astype(BF)

    def to_core(terms, send_buf, recv_buf, own_buf, ssem, rsem):
        cps = []
        for g, (a, b) in enumerate(GROUPS):
            cols = slice(256 * a, 256 * b)
            send_buf[:, :, cols] = terms(64, cols).astype(BF).reshape(4, 16, -1)
            cps.append(send(rcopy(
                send_buf.at[:, :, cols], recv_buf.at[:, :, cols], ssem.at[g], rsem.at[g],
                wid(y, z, 1 - c), x,
            )))
        for a, b in GROUPS:
            cols = slice(256 * a, 256 * b)
            own_buf[:, :, cols] = terms(0, cols).reshape(4, 16, -1)
        return cps

    def along_y(core_cps, own_buf, recv_core, send_buf, recv_buf, ssem, rsem):
        cps = []
        for g, (a, b) in enumerate(GROUPS):
            cols = slice(256 * a, 256 * b)
            core_cps[g].wait_recv()
            for yp in range(4):
                total = own_buf[yp, :, cols] + recv_core[yp, :, cols].astype(F32)
                own_buf[yp, :, cols] = total
                send_buf[yp, :, cols] = total.astype(BF)
            row = []
            for k in (2, 1, 3):
                yt = (y + k) % 4
                i = NG + 3 * g + k - 1
                row.append(send(rcopy(
                    send_buf.at[yt, :, cols], recv_buf.at[k - 1, :, cols], ssem.at[i], rsem.at[i],
                    wid(yt, z, c), x,
                )))
            cps.append(row)
        return cps

    def y_total(cps, g, own_buf, recv_buf):
        cols = slice(256 * GROUPS[g][0], 256 * GROUPS[g][1])
        total = own_buf[y, :, cols]
        for cp in cps[g]:
            cp.wait_recv()
        for k in range(3):
            total = total + recv_buf[k, :, cols].astype(F32)
        return total

    cps = to_core(
        lambda o, cols: dot(heads_all[o : o + 64], wo[:, cols]), d0b, d0r, pown, ss_d, rs_d
    )
    cps = along_y(cps, pown, d0r, d1b, d1r, ss_d, rs_d)
    for g, (a, b) in enumerate(GROUPS):
        cols = slice(256 * a, 256 * b)
        total = y_total(cps, g, pown, d1r)
        att[:, cols] = total
        total = total + resmask[:, cols]
        for j in range(a, b):
            piece = total[:, 256 * (j - a) : 256 * (j - a) + 256]
            asum[j] = piece
            d2b[j] = piece.astype(BF)
            k = (j + 8 - z) % 8
            send(rcopy(d2b.at[j], d2r.at[k], ss_z.at[j], rs_z.at[k], wid(y, j, c), x), z != j)

    zc = lax.min(z, 6)

    @pl.when(z < 7)
    def _():
        mid = asum[zc]
        for k in range(1, 8):
            rcopy(d2b.at[zc], d2r.at[k], ss_z.at[zc], rs_z.at[k], wid(y, (z + k) % 8, c), x).wait_recv()
            mid = mid + d2r[k].astype(F32)
        f1[zc] = (mid * gains[zc]).astype(BF)

    for k in FAR_FIRST:
        zt = (z + k) % 8
        send(rcopy(f1.at[zc], f1.at[zc], ss_f1.at[k - 1], rs_f1.at[zc], wid(y, zt, c), x), z < 7)

    sums = jnp.zeros((16, 1), F32)
    ycps, ccps = [], []
    for g, (a, b) in enumerate(GROUPS):
        for j in range(a, b):
            @pl.when(z != j)
            def _():
                rcopy(f1.at[j], f1.at[j], ss_f1.at[0], rs_f1.at[j], wid(y, j, c), x).wait_recv()
        cols = slice(256 * a, 256 * b)
        x16 = jnp.concatenate([f1[j] for j in range(a, b)], axis=1)
        f2[y, :, cols] = x16
        plain = x16.astype(F32) * gain_inv[:, cols]
        sums = sums + jnp.sum(plain * plain, axis=1, keepdims=True)
        if g == NG - 1:
            high = sums.astype(BF).astype(F32)
            tag = jnp.where(iota((16, 128), 1) < 64, high, sums - high)
            f2[y, :, COLS : COLS + 128] = tag.astype(BF)
            cols = slice(256 * a, COLS + 128)
        row = []
        for k in (2, 1, 3):
            yt = (y + k) % 4
            i = 3 * g + k - 1
            row.append(send(rcopy(
                f2.at[y, :, cols], f2.at[y, :, cols], ss_f2.at[i], rs_f2.at[i], wid(yt, z, c), x
            )))
        ycps.append(row)
        ccps.append([send(rcopy(
            f2.at[y, :, cols], f3.at[y, :, cols], ss_f3.at[4 * g], rs_f3.at[4 * g],
            wid(y, z, 1 - c), x,
        ))])

    need(l_wg)
    need(l_wu)

    def gate_up(rows, acc, cols):
        act = rows[:, :, cols].reshape(64, -1)
        new = [dot_nt(act, wg[:, cols]), dot_nt(act, wu[:, cols])]
        return new if acc is None else [p + q for p, q in zip(acc, new)]

    def to_x(rows, acc, first):
        tag = rows[:, :, COLS:].reshape(64, 128)
        gate, up = acc[0].astype(BF), acc[1].astype(BF)
        for i in range(2):
            b = first + i
            part = slice(32 * i, 32 * i + 32)
            g1b[b, :, 256:384] = tag[part]
            g1b[b, :, 640:768] = tag[part]
            g1b[b, :, 0:288] = gate[part]
            g1b[b, :, 384:672] = up[part]
            k = (b + 4 - x) % 4
            send(rcopy(g1b.at[b], g1r.at[k], ss_g.at[b], rs_g.at[k], w, b), x != b)

    acc = None
    for g, (a, b) in enumerate(GROUPS):
        cols = slice(256 * a, 256 * b)
        full = slice(256 * a, COLS + 128) if g == NG - 1 else cols
        for n, k in enumerate((2, 1, 3)):
            ycps[g][n].wait_recv()
            yb = (y + 4 - k) % 4
            i = 4 * g + k
            ccps[g].append(send(rcopy(
                f2.at[yb, :, full], f3.at[yb, :, full], ss_f3.at[i], rs_f3.at[i],
                wid(y, z, 1 - c), x,
            )))
        acc = gate_up(f2, acc, cols)
    to_x(f2, acc, 0)
    acc = None
    for g, (a, b) in enumerate(GROUPS):
        for cp in ccps[g]:
            cp.wait_recv()
        acc = gate_up(f3, acc, slice(256 * a, 256 * b))
    to_x(f3, acc, 2)
    total = g1b[x].astype(F32)
    for k in range(1, 4):
        rcopy(g1b.at[0], g1r.at[k], ss_g.at[0], rs_g.at[k], w, (x + k) % 4).wait_recv()
        total = total + g1r[k].astype(F32)
    square = total[:, 288:289] + total[:, 320:321]
    norm = lax.rsqrt(square / D + 1e-06)
    gate = total[:, 0:288] * norm
    up = total[:, 384:672] * norm
    hid[x] = (gate / (1.0 + jnp.exp(-gate)) * up).astype(BF)
    cps = []
    for k in (2, 1, 3):
        xt = (x + k) % 4
        cp = rcopy(hid.at[x], hid.at[x], ss_x.at[k - 1], rs_x.at[k - 1], w, xt)
        cps.append(send(cp))
    need(l_wd)
    for cp in cps:
        cp.wait_recv()

    hidden = hid[...].reshape(128, 288)
    cps = to_core(
        lambda o, cols: dot(hidden[o : o + 64], wd[:, cols]), h0b, h0r, pown2, ss_h, rs_h
    )
    cps = along_y(cps, pown2, h0r, h1b, h1r, ss_h, rs_h)
    zcps = []
    for g, (a, b) in enumerate(GROUPS):
        cols = slice(256 * a, 256 * b)
        total = y_total(cps, g, pown2, h1r) + att[:, cols]
        for zp in range(8):
            piece = total[2 * zp : 2 * zp + 2]
            h2f[zp, :, cols] = piece
            h2b[zp, :, cols] = piece.astype(BF)
        row = []
        for k in FAR_FIRST:
            zt = (z + k) % 8
            i = 7 * g + k - 1
            row.append(send(rcopy(
                h2b.at[zt, :, cols], h2r.at[k - 1, :, cols], ss_o.at[i], rs_o.at[i],
                wid(y, zt, c), x,
            )))
        zcps.append(row)
    for g, (a, b) in enumerate(GROUPS):
        cols = slice(256 * a, 256 * b)
        total = res[:, cols].astype(F32) + h2f[z, :, cols]
        for cp in zcps[g]:
            cp.wait_recv()
        for k in range(7):
            total = total + h2r[k, :, cols].astype(F32)
        out[:, cols] = total.astype(BF)

    finish()


def shards(
    residual_in, query_nope, query_rope, absorb_key, absorb_value, latent_cache, cache_lengths,
    slot_rows, out_proj, norm_gain, gate_weight, up_weight, down_weight,
):
    v = pltpu.VMEM
    sem = pltpu.SemaphoreType.DMA
    scratch = [
        v((1, 128), jnp.int32), v((COLS,), BF), v((2, COLS), BF), v((2, 16, 64), BF),
        v((16, 128, 512), BF), v((16, 512, 128), BF), v((2, 576, 2048), BF), v((128, COLS), BF),
        v((288, COLS), BF), v((288, COLS), BF), v((288, COLS), BF), sem((12,)),
        v((8, 3, 16, 128), BF), v((8, 3, 16, 128), BF), v((8, 3, 16, 128), BF),
        sem((7,)), sem((7,)), sem((7,)), sem((7,)),
        v((8, 4, 128), F32), v((8, 4, 128), F32), v((32, 128), F32), v((2, 16, 128), BF),
        v((8, 16, 128), BF), sem((7,)), sem((7,)), sem((8,)), sem((8,)),
        v((128, 128), BF), v((7, 1, 256), F32), v((1, COLS), F32), v((16, COLS), F32),
        v((4, 16, COLS), BF), v((4, 16, COLS), BF), v((4, 16, COLS), F32), v((4, 16, COLS), BF),
        v((3, 16, COLS), BF), v((16, COLS), F32), sem((4 * NG,)), sem((4 * NG,)),
        v((7, 16, 256), F32), v((7, 16, 256), BF), v((8, 16, 256), BF), sem((7,)), sem((8,)),
        v((7, 16, 256), BF), v((4, 16, COLS + 128), BF), v((4, 16, COLS + 128), BF),
        sem((7,)), sem((7,)), sem((3 * NG,)), sem((3 * NG,)), sem((4 * NG,)), sem((4 * NG,)),
        v((4, 32, 768), BF), v((4, 32, 768), BF), v((4, 32, 288), BF),
        sem((4,)), sem((4,)), sem((3,)), sem((3,)),
        v((4, 16, COLS), BF), v((4, 16, COLS), BF), v((4, 16, COLS), F32), v((4, 16, COLS), BF),
        v((3, 16, COLS), BF), sem((4 * NG,)), sem((4 * NG,)),
        v((8, 2, COLS), BF), v((8, 2, COLS), F32), v((7, 2, COLS), BF),
        sem((7 * NG,)), sem((7 * NG,)),
    ]
    return pl.pallas_call(
        kernel,
        out_shape=jax.ShapeDtypeStruct((2, COLS), BF),
        in_specs=[SMEM, SMEM] + [HBM] * 12,
        out_specs=VM,
        scratch_shapes=scratch,
        compiler_params=pltpu.CompilerParams(
            collective_id=0, has_side_effects=True, vmem_limit_bytes=67043328
        ),
    )(
        slot_rows, cache_lengths, slot_rows.reshape(1, 128), norm_gain,
        residual_in, query_nope, query_rope, absorb_key, absorb_value,
        jnp.swapaxes(latent_cache, 1, 2), out_proj, gate_weight.T, up_weight.T, down_weight,
    )


def solution(mesh):
    in_specs = (
        P("wide", "narrow"),
        P("wide", "narrow", None),
        P("wide", "narrow", None),
        P("narrow", None, None),
        P("narrow", None, None),
        P("wide", None, None),
        P("wide"),
        P(),
        P("wide", "narrow"),
        P("narrow"),
        P("narrow", "wide"),
        P("narrow", "wide"),
        P("wide", "narrow"),
    )
    out_specs = P("wide", "narrow")
    return jax.shard_map(shards, mesh=mesh, in_specs=in_specs, out_specs=out_specs, check_vma=False)
```

time: 91.9 us -> 76.7 us (0.83)
  local copies, waits for them, and re-layouts: 13.8 us -> 1.29 us
  Pallas kernels: 77.7 us -> 75.4 us
    unnamed x18 -> x1, local copies, waits for them, and re-layouts: 13.1 us -> 1.29 us
    pallas_call x1, Pallas kernels: 77.7 us -> 75.4 us  [shards(): pl.pallas_call(kernel, out_shape=jax.ShapeDtypeStruct((2, COLS), BF), in_...]
where the time goes in v2:
time: 76.7 us
  Pallas kernels  75.4 us (98%)
  local copies, waits for them, and re-layouts  1.29 us (2%)
    pallas_call x1, Pallas kernels, shards(): pl.pallas_call(kernel, out_shape=jax.ShapeDtypeStruct((2, COLS), BF), in_...  75.4 us

profile of v2, /device:TPU:1, one launch (start us, length us, event | category | flops | bytes accessed | tf_op | source)
XLA Modules:
  0.0 76.7 jit_solution(13429650733855640783)
XLA Ops:
  0.0 75.4 %shard_map.127 = bf16[2,1792]{1,0:T(2,128)(2,1)} custom-call(s32[128]{0:T(128)} %slots.1, s32[2]{0:T(128)} %lengths.1, s32[1,128]{1,0:T(1,128)} %bitcast.7, bf16[1792]{0:T(1024)(128)(2,1)} %gain_h.1, bf16[2,1792]{1,0:T(2,128)(2,1)} %res_h.1, bf16[2,16,128]{2,1,0:T(8,128)(2,1)} %qn_h.1, bf16[2,16,64]{2,1,0:T(8,128)(2,1)} %qr_h.1, bf16[16,128,512]{2,1,0:T(8,128)(2,1)} %ak_h.1, ...), custom_call_target="tpu_custom_call" | custom-call | tf_op jit(solution)/shard_map/pallas_call | solution.py:482
  75.4 1.3 %copy.15 = bf16[2,1792]{1,0:T(2,128)(2,1)} copy(bf16[2,1792]{1,0:T(2,128)(2,1)} %shard_map.127) | data formatting | bytes 14336

commit v3 on v2

v3 whole, which is shorter than its diff:
```python
import math

import jax
import jax.numpy as jnp
from jax import lax
from jax.experimental import pallas as pl
from jax.experimental.pallas import tpu as pltpu
from jax.sharding import PartitionSpec as P

D = 7168
MESH = pl.DeviceIdType.MESH
F32 = jnp.float32
BF = jnp.bfloat16
COLS = 1792
GROUPS = ((0, 2), (2, 4), (4, 7))
NG = len(GROUPS)
FAR_FIRST = (4, 3, 5, 2, 6, 1, 7)
SCALE = 1.0 / math.sqrt(192)
HBM = pl.BlockSpec(memory_space=pltpu.HBM)
SMEM = pl.BlockSpec(memory_space=pltpu.SMEM)
VM = pl.BlockSpec(memory_space=pltpu.VMEM)


def dot(a, b):
    return jnp.dot(a, b, preferred_element_type=F32)


def dot_nt(a, b):
    return lax.dot_general(a, b, (((1,), (1,)), ((), ())), preferred_element_type=F32)


def iota(shape, axis):
    return lax.broadcasted_iota(jnp.int32, shape, axis)


def swap_halves(tile):
    return jnp.concatenate([tile[:, 64:], tile[:, :64]], axis=1)


def kernel(
    slots, lengths, slot_vec_h, gain_h,
    res_h, qn_h, qr_h, ak_h, av_h, kv_h, wo_h, wg_h, wu_h, wd_h,
    out,
    slot_vec, gain_v, res, qr, ak, av, kv, wo, wg, wu, wd, lsem,
    relay, gq, sq, rq, ss_a, rs_a, hs, hb, hf, ss_c, rs_c,
    pm, gains, gain_inv, resmask,
    d0b, d0r, pown, d1b, d1r, att, ss_d, rs_d, asum, d2b, d2r, ss_z, rs_z,
    f1, f2, f3, ss_f1, rs_f1, ss_f2, rs_f2, rs_f3,
    g1b, g1r, hid, ss_g, rs_g,
    h0b, h0r, pown2, h1b, h1r, ss_h, rs_h, h2b, h2f, h2r, ss_o, rs_o,
):
    w = lax.axis_index("wide")
    x = lax.axis_index("narrow")
    y, z, c = w // 16, (w // 2) % 8, w % 2
    yc = y * 2 + c

    def wid(y_, z_, c_):
        return y_ * 16 + z_ * 2 + c_

    def rcopy(src, dst, ssem, rsem, w_, x_):
        return pltpu.make_async_remote_copy(
            src_ref=src, dst_ref=dst, send_sem=ssem, recv_sem=rsem,
            device_id=(w_, x_), device_id_type=MESH,
        )

    loads, held = [], []

    def load(src, dst):
        cp = pltpu.make_async_copy(src, dst, lsem.at[len(loads)])
        cp.start()
        loads.append(cp)
        held.append(cp)
        return cp

    def need(cp):
        held[:] = [h for h in held if h is not cp]
        cp.wait()

    drains = []

    def finish():
        for cp in held:
            cp.wait()
        for cond, cp in drains:
            if cond is None:
                cp.wait_send()
            else:
                @pl.when(cond)
                def _():
                    cp.wait_send()

    def send(cp, cond=None):
        if cond is None:
            cp.start()
        else:
            @pl.when(cond)
            def _():
                cp.start()

    def arrivals(ref, sem):
        rcopy(ref, ref, sem, sem, w, (x + 1) % 4).wait_recv()

    def drain(ref, sem, cond=None):
        drains.append((cond, rcopy(ref, ref, sem, sem, w, (x + 1) % 4)))

    bar = pltpu.get_barrier_semaphore()

    def greet(w_, x_):
        pl.semaphore_signal(bar, inc=1, device_id=(w_, x_), device_id_type=MESH)

    for k in range(1, 8):
        t = (yc + k) % 8
        greet(wid(t // 2, z, t % 2), x)
    for k in (1, 7):
        greet(wid(y, (z + k) % 8, c), x)
    for k in range(1, 4):
        greet(w, (x + k) % 4)
    l_qn = load(qn_h, gq.at[yc, pl.ds(0, 2)])
    l_qr = load(qr_h, qr)
    l_ak = load(ak_h, ak)
    l_sv = load(slot_vec_h, slot_vec)
    l_gain = load(gain_h, gain_v)
    l_res = load(res_h, res)
    l_kv = load(kv_h, kv)
    l_av = load(av_h, av)
    l_wo = load(wo_h, wo)
    l_wg = load(wg_h, wg)
    l_wu = load(wu_h, wu)
    l_wd = load(wd_h, wd)

    pl.semaphore_wait(bar, 12)
    need(l_qr)
    gq[yc, 2] = jnp.concatenate([qr[0], qr[1]], axis=1)
    need(l_qn)
    for k in (4, 5, 2, 3, 6, 7, 1):
        t = (yc + k) % 8
        send(rcopy(gq.at[yc], gq.at[yc], ss_a.at[0], rs_a.at[0], wid(t // 2, z, t % 2), x))
    drain(gq.at[0:7], ss_a.at[0])

    def hand_on(i):
        for k in (1, 7):
            pl.semaphore_signal(
                relay.at[i], inc=1, device_id=(wid(y, (z + k) % 8, c), x), device_id_type=MESH
            )

    hand_on(0)

    need(l_sv)
    sv = slot_vec[...]
    srow = (sv & 2) * 32 + (sv // 32) * 16 + ((sv // 4) & 7) * 2 + (sv & 1)
    rho = iota((128, 128), 0)
    own_first = jnp.where(rho < 64, rho + 64 * c, rho - 64 * c)
    hot = jnp.where(srow == own_first, 1.0, 0.0).astype(BF)
    pm[...] = hot
    pl.semaphore_wait(relay.at[0], 2)
    hand_on(1)
    need(l_res)
    resf = res[...].astype(F32)
    spread = jnp.concatenate([resf] * 8, axis=0)
    resmask[...] = jnp.where(iota((16, COLS), 0) // 2 == z, spread, 0.0)
    need(l_gain)
    gfull = gain_v[...].astype(F32).reshape(1, COLS)
    for j in range(7):
        gains[j] = gfull[:, 256 * j : 256 * j + 256]
    gain_inv[...] = 1.0 / gfull
    r32 = iota((32, 32), 0)
    c32 = iota((32, 32), 1)
    by_dest = jnp.where(c32 == (r32 & 1) * 16 + (r32 // 4) * 2 + ((r32 // 2) & 1), 1.0, 0.0).astype(BF)
    pl.semaphore_wait(relay.at[1], 2)
    hand_on(2)
    pl.semaphore_wait(relay.at[2], 2)

    arrivals(gq.at[0:7], rs_a.at[0])

    low = iota((16, 128), 1) < 64
    for zp in range(8):
        ropes = []
        for s in range(2):
            r = slots[wid(y, zp, c) * 2 + s]
            i8 = (r // 32) * 2 + ((r // 2) & 1)
            i = r & 1
            sq[zp, s] = gq[i8, i]
            tile = gq[i8, 2].astype(F32)
            ropes.append(jnp.where(i == s, tile, swap_halves(tile)))
        sq[zp, 2] = jnp.where(low, ropes[0], ropes[1]).astype(BF)
    for k in FAR_FIRST:
        zt = (z + k) % 8
        send(rcopy(sq.at[zt], rq.at[z], ss_a.at[1], rs_a.at[1], wid(y, zt, c), x))
    drain(sq.at[0:7], ss_a.at[1])
    rq[z] = sq[z]
    need(l_ak)
    need(l_kv)
    arrivals(rq.at[0:7], rs_a.at[1])

    q_parts, ropes = [], []
    for s in range(2):
        r = slots[w * 2 + s]
        zr = (r // 4) & 7
        q_parts.append(rq[zr, s])
        ropes.append(rq[zr, 2][:, 64 * s : 64 * s + 64])
    qn = jnp.concatenate(q_parts, axis=0)
    wide_q = jnp.concatenate([qn] * 16, axis=1)
    own_head = iota((32, 2048), 1) // 128 == (iota((32, 2048), 0) & 15)
    wide_q = jnp.where(own_head, wide_q, jnp.zeros_like(wide_q))
    qlat = dot(wide_q, ak[...].reshape(2048, 512)).astype(BF)
    ctxs = []
    for s in range(2):
        sc = dot(qlat[16 * s : 16 * s + 16], kv[s, 0:512])
        sc = (sc + dot(ropes[s], kv[s, 512:576])) * SCALE
        live = iota((16, 2048), 1) < lengths[s]
        sc = jnp.where(live, sc, -1e30)
        e = jnp.exp(sc - jnp.max(sc, axis=1, keepdims=True))
        e = jnp.where(live, e, 0.0)
        p = (e / jnp.sum(e, axis=1, keepdims=True)).astype(BF)
        ctxs.append(dot_nt(p, kv[s, 0:512]).astype(BF))
    ctx = jnp.concatenate(ctxs, axis=0)
    wide_c = jnp.concatenate([ctx] * 16, axis=1)
    own_head = iota((32, 8192), 1) // 512 == (iota((32, 8192), 0) & 15)
    wide_c = jnp.where(own_head, wide_c, jnp.zeros_like(wide_c))
    need(l_av)
    heads = dot(wide_c, av[...].reshape(8192, 128)).astype(BF)

    hp = dot(by_dest, heads)
    for h in range(16):
        hs[h] = hp[2 * h : 2 * h + 2].astype(BF)
    home = x == y
    for kh in (8, 7, 9, 6, 10, 5, 11, 4, 12, 3, 13, 2, 14, 1, 15, 0):
        h = (2 * z + c + kh) % 16
        for kx in (2, 1, 3, 0):
            cp = rcopy(hs.at[h], hb.at[w], ss_c.at[0], rs_c.at[0], x * 16 + h, (x + kx) % 4)
            send(cp, x != y if kx == 0 and kh == 0 else None)
    drain(hb.at[0:63], ss_c.at[0], home)
    drain(hb.at[0:64], ss_c.at[0], jnp.logical_not(home))

    @pl.when(home)
    def _():
        hb[w] = hs[2 * z + c]
        arrivals(hb.at[0:63], rs_c.at[0])

    @pl.when(jnp.logical_not(home))
    def _():
        arrivals(hb.at[0:64], rs_c.at[0])

    for j in range(64):
        hf[2 * j : 2 * j + 2] = hb[j].astype(F32)
    need(l_wo)
    heads_all = dot(pm[...], hf[...].astype(BF)).astype(BF)

    def to_core(terms, send_buf, recv_buf, own_buf, sems, rsem):
        for g, (a, b) in enumerate(GROUPS):
            cols = slice(256 * a, 256 * b)
            send_buf[:, :, cols] = terms(64, cols).astype(BF).reshape(4, 16, -1)
            send(rcopy(
                send_buf.at[:, :, cols], recv_buf.at[:, :, cols], sems.at[0], rsem.at[g],
                wid(y, z, 1 - c), x,
            ))
        drain(send_buf.at[0:4], sems.at[0])
        for a, b in GROUPS:
            cols = slice(256 * a, 256 * b)
            own_buf[:, :, cols] = terms(0, cols).reshape(4, 16, -1)

    def along_y(own_buf, recv_core, send_buf, recv_buf, sems, rsem):
        for g, (a, b) in enumerate(GROUPS):
            cols = slice(256 * a, 256 * b)
            arrivals(recv_core.at[:, :, cols], rsem.at[g])
            for yp in range(4):
                total = own_buf[yp, :, cols] + recv_core[yp, :, cols].astype(F32)
                own_buf[yp, :, cols] = total
                send_buf[yp, :, cols] = total.astype(BF)
            for k in (2, 1, 3):
                yt = (y + k) % 4
                send(rcopy(
                    send_buf.at[yt, :, cols], recv_buf.at[k - 1, :, cols], sems.at[1],
                    rsem.at[NG + g], wid(yt, z, c), x,
                ))
        drain(send_buf.at[0:3], sems.at[1])

    def y_total(g, own_buf, recv_buf, rsem):
        cols = slice(256 * GROUPS[g][0], 256 * GROUPS[g][1])
        total = own_buf[y, :, cols]
        arrivals(recv_buf.at[:, :, cols], rsem.at[NG + g])
        for k in range(3):
            total = total + recv_buf[k, :, cols].astype(F32)
        return total

    to_core(lambda o, cols: dot(heads_all[o : o + 64], wo[:, cols]), d0b, d0r, pown, ss_d, rs_d)
    along_y(pown, d0r, d1b, d1r, ss_d, rs_d)
    for g, (a, b) in enumerate(GROUPS):
        cols = slice(256 * a, 256 * b)
        total = y_total(g, pown, d1r, rs_d)
        att[:, cols] = total
        total = total + resmask[:, cols]
        for j in range(a, b):
            piece = total[:, 256 * (j - a) : 256 * (j - a) + 256]
            asum[j] = piece
            d2b[j] = piece.astype(BF)
            k = (j + 8 - z) % 8
            send(rcopy(d2b.at[j], d2r.at[k], ss_z.at[0], rs_z.at[0], wid(y, j, c), x), z != j)
    drain(d2b.at[0:6], ss_z.at[0], z < 7)
    drain(d2b.at[0:7], ss_z.at[0], z == 7)

    zc = lax.min(z, 6)

    @pl.when(z < 7)
    def _():
        mid = asum[zc]
        arrivals(d2r.at[1:8], rs_z.at[0])
        for k in range(1, 8):
            mid = mid + d2r[k].astype(F32)
        f1[zc] = (mid * gains[zc]).astype(BF)

    zg = sum(jnp.where(zc >= b, 1, 0) for _, b in GROUPS[:-1])
    for k in FAR_FIRST:
        zt = (z + k) % 8
        send(rcopy(f1.at[zc], f1.at[zc], ss_f1.at[0], rs_f1.at[zg], wid(y, zt, c), x), z < 7)
    drain(f1.at[0:7], ss_f1.at[0], z < 7)

    sums = jnp.zeros((16, 1), F32)
    for g, (a, b) in enumerate(GROUPS):
        mine = jnp.logical_and(z >= a, z < b)

        @pl.when(jnp.logical_not(mine))
        def _():
            arrivals(f1.at[a:b], rs_f1.at[g])

        if b - a > 1:
            @pl.when(mine)
            def _():
                arrivals(f1.at[a : b - 1], rs_f1.at[g])

        cols = slice(256 * a, 256 * b)
        x16 = jnp.concatenate([f1[j] for j in range(a, b)], axis=1)
        f2[y, :, cols] = x16
        plain = x16.astype(F32) * gain_inv[:, cols]
        sums = sums + jnp.sum(plain * plain, axis=1, keepdims=True)
        if g == NG - 1:
            high = sums.astype(BF).astype(F32)
            tag = jnp.where(iota((16, 128), 1) < 64, high, sums - high)
            f2[y, :, COLS : COLS + 128] = tag.astype(BF)
            cols = slice(256 * a, COLS + 128)
        for k in (2, 1, 3):
            yt = (y + k) % 4
            send(rcopy(
                f2.at[y, :, cols], f2.at[y, :, cols], ss_f2.at[0], rs_f2.at[g], wid(yt, z, c), x
            ))
        send(rcopy(
            f2.at[y, :, cols], f3.at[y, :, cols], ss_f2.at[1], rs_f3.at[g], wid(y, z, 1 - c), x
        ))
    drain(f2.at[0:3], ss_f2.at[0])
    drain(f2.at[0:4], ss_f2.at[1])

    need(l_wg)
    need(l_wu)

    def gate_up(rows, acc, cols):
        act = rows[:, :, cols].reshape(64, -1)
        new = [dot_nt(act, wg[:, cols]), dot_nt(act, wu[:, cols])]
        return new if acc is None else [p + q for p, q in zip(acc, new)]

    def to_x(rows, acc, first):
        tag = rows[:, :, COLS:].reshape(64, 128)
        gate, up = acc[0].astype(BF), acc[1].astype(BF)
        for i in range(2):
            b = first + i
            part = slice(32 * i, 32 * i + 32)
            g1b[b, :, 256:384] = tag[part]
            g1b[b, :, 640:768] = tag[part]
            g1b[b, :, 0:288] = gate[part]
            g1b[b, :, 384:672] = up[part]
            k = (b + 4 - x) % 4
            send(rcopy(g1b.at[b], g1r.at[k], ss_g.at[0], rs_g.at[0], w, b), x != b)

    acc = None
    for g, (a, b) in enumerate(GROUPS):
        cols = slice(256 * a, 256 * b)
        full = slice(256 * a, COLS + 128) if g == NG - 1 else cols
        arrivals(f2.at[0:3, :, full], rs_f2.at[g])
        for k in (2, 1, 3):
            yb = (y + 4 - k) % 4
            send(rcopy(
                f2.at[yb, :, full], f3.at[yb, :, full], ss_f2.at[1], rs_f3.at[g],
                wid(y, z, 1 - c), x,
            ))
        acc = gate_up(f2, acc, cols)
    to_x(f2, acc, 0)
    acc = None
    for g, (a, b) in enumerate(GROUPS):
        full = slice(256 * a, COLS + 128) if g == NG - 1 else slice(256 * a, 256 * b)
        arrivals(f3.at[:, :, full], rs_f3.at[g])
        acc = gate_up(f3, acc, slice(256 * a, 256 * b))
    to_x(f3, acc, 2)
    drain(g1b.at[0:3], ss_g.at[0])
    total = g1b[x].astype(F32)
    arrivals(g1r.at[1:4], rs_g.at[0])
    for k in range(1, 4):
        total = total + g1r[k].astype(F32)
    square = total[:, 288:289] + total[:, 320:321]
    norm = lax.rsqrt(square / D + 1e-06)
    gate = total[:, 0:288] * norm
    up = total[:, 384:672] * norm
    hid[x] = (gate / (1.0 + jnp.exp(-gate)) * up).astype(BF)
    for k in (2, 1, 3):
        send(rcopy(hid.at[x], hid.at[x], ss_g.at[1], rs_g.at[1], w, (x + k) % 4))
    drain(hid.at[0:3], ss_g.at[1])
    need(l_wd)
    arrivals(hid.at[0:3], rs_g.at[1])

    hidden = hid[...].reshape(128, 288)
    to_core(lambda o, cols: dot(hidden[o : o + 64], wd[:, cols]), h0b, h0r, pown2, ss_h, rs_h)
    along_y(pown2, h0r, h1b, h1r, ss_h, rs_h)
    for g, (a, b) in enumerate(GROUPS):
        cols = slice(256 * a, 256 * b)
        total = y_total(g, pown2, h1r, rs_h) + att[:, cols]
        for zp in range(8):
            piece = total[2 * zp : 2 * zp + 2]
            h2f[zp, :, cols] = piece
            h2b[zp, :, cols] = piece.astype(BF)
        for k in FAR_FIRST:
            zt = (z + k) % 8
            send(rcopy(
                h2b.at[zt, :, cols], h2r.at[k - 1, :, cols], ss_o.at[0], rs_o.at[g],
                wid(y, zt, c), x,
            ))
    drain(h2b.at[0:7], ss_o.at[0])
    for g, (a, b) in enumerate(GROUPS):
        cols = slice(256 * a, 256 * b)
        total = res[:, cols].astype(F32) + h2f[z, :, cols]
        arrivals(h2r.at[:, :, cols], rs_o.at[g])
        for k in range(7):
            total = total + h2r[k, :, cols].astype(F32)
        out[:, cols] = total.astype(BF)

    finish()


def shards(
    residual_in, query_nope, query_rope, absorb_key, absorb_value, latent_cache, cache_lengths,
    slot_rows, out_proj, norm_gain, gate_weight, up_weight, down_weight,
):
    v = pltpu.VMEM
    sem = pltpu.SemaphoreType.DMA
    scratch = [
        v((1, 128), jnp.int32), v((COLS,), BF), v((2, COLS), BF), v((2, 16, 64), BF),
        v((16, 128, 512), BF), v((16, 512, 128), BF), v((2, 576, 2048), BF), v((128, COLS), BF),
        v((288, COLS), BF), v((288, COLS), BF), v((288, COLS), BF), sem((12,)),
        pltpu.SemaphoreType.REGULAR((3,)),
        v((8, 3, 16, 128), BF), v((8, 3, 16, 128), BF), v((8, 3, 16, 128), BF), sem((2,)), sem((2,)),
        v((16, 2, 128), BF), v((64, 2, 128), BF), v((128, 128), F32), sem((1,)), sem((1,)),
        v((128, 128), BF), v((7, 1, 256), F32), v((1, COLS), F32), v((16, COLS), F32),
        v((4, 16, COLS), BF), v((4, 16, COLS), BF), v((4, 16, COLS), F32), v((4, 16, COLS), BF),
        v((3, 16, COLS), BF), v((16, COLS), F32), sem((2,)), sem((2 * NG,)),
        v((7, 16, 256), F32), v((7, 16, 256), BF), v((8, 16, 256), BF), sem((1,)), sem((1,)),
        v((7, 16, 256), BF), v((4, 16, COLS + 128), BF), v((4, 16, COLS + 128), BF),
        sem((1,)), sem((NG,)), sem((2,)), sem((NG,)), sem((NG,)),
        v((4, 32, 768), BF), v((4, 32, 768), BF), v((4, 32, 288), BF),
        sem((2,)), sem((2,)),
        v((4, 16, COLS), BF), v((4, 16, COLS), BF), v((4, 16, COLS), F32), v((4, 16, COLS), BF),
        v((3, 16, COLS), BF), sem((2,)), sem((2 * NG,)),
        v((8, 2, COLS), BF), v((8, 2, COLS), F32), v((7, 2, COLS), BF),
        sem((1,)), sem((NG,)),
    ]
    return pl.pallas_call(
        kernel,
        out_shape=jax.ShapeDtypeStruct((2, COLS), BF),
        in_specs=[SMEM, SMEM] + [HBM] * 12,
        out_specs=VM,
        scratch_shapes=scratch,
        compiler_params=pltpu.CompilerParams(
            collective_id=0, has_side_effects=True, vmem_limit_bytes=67043328
        ),
    )(
        slot_rows, cache_lengths, slot_rows.reshape(1, 128), norm_gain,
        residual_in, query_nope, query_rope, absorb_key, absorb_value,
        jnp.swapaxes(latent_cache, 1, 2), out_proj, gate_weight.T, up_weight.T, down_weight,
    )


def solution(mesh):
    in_specs = (
        P("wide", "narrow"),
        P("wide", "narrow", None),
        P("wide", "narrow", None),
        P("narrow", None, None),
        P("narrow", None, None),
        P("wide", None, None),
        P("wide"),
        P(),
        P("wide", "narrow"),
        P("narrow"),
        P("narrow", "wide"),
        P("narrow", "wide"),
        P("wide", "narrow"),
    )
    out_specs = P("wide", "narrow")
    return jax.shard_map(shards, mesh=mesh, in_specs=in_specs, out_specs=out_specs, check_vma=False)
```

time: 76.7 us -> 71.4 us (0.931)
  Pallas kernels: 75.4 us -> 69.9 us
    pallas_call x1, Pallas kernels: 75.4 us -> 69.9 us  [shards(): pl.pallas_call(kernel, out_shape=jax.ShapeDtypeStruct((2, COLS), BF), in_...]
where the time goes in v3:
time: 71.4 us; the launch traced here: 71.2 us
  Pallas kernels  69.9 us (98%)
  local copies, waits for them, and re-layouts  1.29 us (2%)
    pallas_call x1, Pallas kernels, shards(): pl.pallas_call(kernel, out_shape=jax.ShapeDtypeStruct((2, COLS), BF), in_...  69.9 us

profile of v3, /device:TPU:1, one launch (start us, length us, event | category | flops | bytes accessed | tf_op | source)
XLA Modules:
  0.0 71.2 jit_solution(6036779283722138847)
XLA Ops:
  0.0 69.9 %shard_map.127 = bf16[2,1792]{1,0:T(2,128)(2,1)} custom-call(s32[128]{0:T(128)} %slots.1, s32[2]{0:T(128)} %lengths.1, s32[1,128]{1,0:T(1,128)} %bitcast.7, bf16[1792]{0:T(1024)(128)(2,1)} %gain_h.1, bf16[2,1792]{1,0:T(2,128)(2,1)} %res_h.1, bf16[2,16,128]{2,1,0:T(8,128)(2,1)} %qn_h.1, bf16[2,16,64]{2,1,0:T(8,128)(2,1)} %qr_h.1, bf16[16,128,512]{2,1,0:T(8,128)(2,1)} %ak_h.1, ...), custom_call_target="tpu_custom_call" | custom-call | tf_op jit(solution)/shard_map/pallas_call | solution.py:462
  69.9 1.3 %copy.15 = bf16[2,1792]{1,0:T(2,128)(2,1)} copy(bf16[2,1792]{1,0:T(2,128)(2,1)} %shard_map.127) | data formatting | bytes 14336

commit v4 on v3

v4 whole, which is shorter than its diff:
```python
import math

import jax
import jax.numpy as jnp
from jax import lax
from jax.experimental import pallas as pl
from jax.experimental.pallas import tpu as pltpu
from jax.sharding import PartitionSpec as P

D = 7168
MESH = pl.DeviceIdType.MESH
F32 = jnp.float32
BF = jnp.bfloat16
COLS = 1792
HALF = COLS // 2
GROUPS = ((0, 1), (1, 3), (3, 5), (5, 7))
NG = len(GROUPS)
FAR_FIRST = (4, 3, 5, 2, 6, 1, 7)
SCALE = 1.0 / math.sqrt(192)
HBM = pl.BlockSpec(memory_space=pltpu.HBM)
SMEM = pl.BlockSpec(memory_space=pltpu.SMEM)
VM = pl.BlockSpec(memory_space=pltpu.VMEM)


def dot(a, b):
    return jnp.dot(a, b, preferred_element_type=F32)


def dot_nt(a, b):
    return lax.dot_general(a, b, (((1,), (1,)), ((), ())), preferred_element_type=F32)


def iota(shape, axis):
    return lax.broadcasted_iota(jnp.int32, shape, axis)


def swap_halves(tile):
    return jnp.concatenate([tile[:, 64:], tile[:, :64]], axis=1)


def kernel(
    slots, lengths, slot_vec_h, gain_h,
    res_h, qn_h, qr_h, ak_h, av_h, kv_h, wo_h, wg_h, wu_h, wd_h,
    out,
    slot_vec, gain_v, res, qr, ak, av, kv, wo, wga, wgb, wua, wub, wd, lsem,
    relay, gq, sq, rq, ss_a, rs_a, hs, hb, hf, ss_c, rs_c,
    pm, gains, inv_own, inv_other, resx, resmask, ss_w, rs_w,
    pown, d1b, d1r, ss_d, rs_d, asum, d2b, d2r, ss_z, rs_z,
    f1, f2, f3, mrow, ss_f1, rs_f1, ss_f2, rs_f2, rs_f3,
    g1b, g1r, hid, ss_g, rs_g,
    h0b, h0r, pown2, h1b, h1r, ss_h, rs_h, h2b, h2f, h2r, ss_o, rs_o,
):
    w = lax.axis_index("wide")
    x = lax.axis_index("narrow")
    y, z, c = w // 16, (w // 2) % 8, w % 2
    yc = y * 2 + c
    own_cols = pl.ds(pl.multiple_of(c * HALF, 128), HALF)
    other_cols = pl.ds(pl.multiple_of((1 - c) * HALF, 128), HALF)

    def wid(y_, z_, c_):
        return y_ * 16 + z_ * 2 + c_

    def rcopy(src, dst, ssem, rsem, w_, x_):
        return pltpu.make_async_remote_copy(
            src_ref=src, dst_ref=dst, send_sem=ssem, recv_sem=rsem,
            device_id=(w_, x_), device_id_type=MESH,
        )

    loads, held = [], []

    def load(src, dst):
        cp = pltpu.make_async_copy(src, dst, lsem.at[len(loads)])
        cp.start()
        loads.append(cp)
        held.append(cp)
        return cp

    def need(cp):
        held[:] = [h for h in held if h is not cp]
        cp.wait()

    drains = []

    def finish():
        for cp in held:
            cp.wait()
        for cond, cp in drains:
            if cond is None:
                cp.wait_send()
            else:
                @pl.when(cond)
                def _():
                    cp.wait_send()

    def send(cp, cond=None):
        if cond is None:
            cp.start()
        else:
            @pl.when(cond)
            def _():
                cp.start()

    def arrivals(ref, sem):
        rcopy(ref, ref, sem, sem, w, (x + 1) % 4).wait_recv()

    def drain(ref, sem, cond=None):
        drains.append((cond, rcopy(ref, ref, sem, sem, w, (x + 1) % 4)))

    bar = pltpu.get_barrier_semaphore()

    def greet(w_, x_):
        pl.semaphore_signal(bar, inc=1, device_id=(w_, x_), device_id_type=MESH)

    for k in range(1, 8):
        t = (yc + k) % 8
        greet(wid(t // 2, z, t % 2), x)
    for k in (1, 7):
        greet(wid(y, (z + k) % 8, c), x)
    for k in range(1, 4):
        greet(w, (x + k) % 4)
    l_qn = load(qn_h, gq.at[yc, pl.ds(0, 2)])
    l_qr = load(qr_h, qr)
    l_ak = load(ak_h, ak)
    l_sv = load(slot_vec_h, slot_vec)
    l_gain = load(gain_h, gain_v)
    l_res = load(res_h, res)
    l_kv = load(kv_h, kv)
    l_av = load(av_h, av)
    l_wo = load(wo_h.at[:, own_cols], wo.at[0:128])
    l_wga = load(wg_h.at[:, own_cols], wga)
    l_wua = load(wu_h.at[:, own_cols], wua)
    l_wgb = load(wg_h.at[:, other_cols], wgb)
    l_wub = load(wu_h.at[:, other_cols], wub)
    l_wd = load(wd_h, wd)

    pl.semaphore_wait(bar, 12)
    need(l_qr)
    gq[yc, 2] = jnp.concatenate([qr[0], qr[1]], axis=1)
    need(l_qn)
    for k in (4, 5, 2, 3, 6, 7, 1):
        t = (yc + k) % 8
        send(rcopy(gq.at[yc], gq.at[yc], ss_a.at[0], rs_a.at[0], wid(t // 2, z, t % 2), x))
    drain(gq.at[0:7], ss_a.at[0])
    partner = wid(y, z, 1 - c)
    send(rcopy(res_h.at[:, other_cols], resx, ss_w.at[0], rs_w.at[0], partner, x))
    send(rcopy(wo_h.at[:, other_cols], wo.at[128:256], ss_w.at[1], rs_w.at[1], partner, x))
    drain(resx, ss_w.at[0])
    drain(wo.at[128:256], ss_w.at[1])

    def hand_on(i):
        for k in (1, 7):
            pl.semaphore_signal(
                relay.at[i], inc=1, device_id=(wid(y, (z + k) % 8, c), x), device_id_type=MESH
            )

    hand_on(0)

    need(l_sv)
    sv = slot_vec[...]
    srow = (sv // 32) * 32 + ((sv // 2) & 1) * 16 + ((sv // 4) & 7) * 2 + (sv & 1)
    pm[...] = jnp.where(srow == iota((128, 128), 0), 1.0, 0.0).astype(BF)
    pl.semaphore_wait(relay.at[0], 2)
    hand_on(1)
    need(l_res)
    need(l_gain)
    gfull = gain_v[...].astype(F32).reshape(1, COLS)
    left, right = gfull[:, :HALF], gfull[:, HALF:]
    gain_own = jnp.where(c == 0, left, right)
    inv_own[...] = 1.0 / gain_own
    inv_other[...] = 1.0 / jnp.where(c == 0, right, left)
    for j in range(7):
        gains[j] = gain_own[:, 128 * j : 128 * j + 128]
    r32 = iota((32, 32), 0)
    c32 = iota((32, 32), 1)
    by_dest = jnp.where(c32 == (r32 & 1) * 16 + (r32 // 4) * 2 + ((r32 // 2) & 1), 1.0, 0.0).astype(BF)
    pl.semaphore_wait(relay.at[1], 2)
    hand_on(2)
    pl.semaphore_wait(relay.at[2], 2)

    arrivals(gq.at[0:7], rs_a.at[0])

    low = iota((16, 128), 1) < 64
    for zp in range(8):
        ropes = []
        for s in range(2):
            r = slots[wid(y, zp, c) * 2 + s]
            i8 = (r // 32) * 2 + ((r // 2) & 1)
            i = r & 1
            sq[zp, s] = gq[i8, i]
            tile = gq[i8, 2].astype(F32)
            ropes.append(jnp.where(i == s, tile, swap_halves(tile)))
        sq[zp, 2] = jnp.where(low, ropes[0], ropes[1]).astype(BF)
    for k in FAR_FIRST:
        zt = (z + k) % 8
        send(rcopy(sq.at[zt], rq.at[z], ss_a.at[1], rs_a.at[1], wid(y, zt, c), x))
    drain(sq.at[0:7], ss_a.at[1])
    rq[z] = sq[z]
    arrivals(resx, rs_w.at[0])
    mine = jnp.where(c == 0, res[:, :HALF], res[:, HALF:]).astype(F32)
    theirs = resx[...].astype(F32)
    top = jnp.where(c == 0, mine, theirs)
    low2 = jnp.where(c == 0, theirs, mine)
    spread = jnp.concatenate([top] * 8 + [low2] * 8, axis=0)
    resmask[...] = jnp.where((iota((32, HALF), 0) // 2) % 8 == z, spread, 0.0)
    need(l_ak)
    need(l_kv)
    arrivals(rq.at[0:7], rs_a.at[1])

    q_parts, ropes = [], []
    for s in range(2):
        r = slots[w * 2 + s]
        zr = (r // 4) & 7
        q_parts.append(rq[zr, s])
        ropes.append(rq[zr, 2][:, 64 * s : 64 * s + 64])
    qn = jnp.concatenate(q_parts, axis=0)
    wide_q = jnp.concatenate([qn] * 16, axis=1)
    own_head = iota((32, 2048), 1) // 128 == (iota((32, 2048), 0) & 15)
    wide_q = jnp.where(own_head, wide_q, jnp.zeros_like(wide_q))
    qlat = dot(wide_q, ak[...].reshape(2048, 512)).astype(BF)
    ctxs = []
    for s in range(2):
        sc = dot(qlat[16 * s : 16 * s + 16], kv[s, 0:512])
        sc = (sc + dot(ropes[s], kv[s, 512:576])) * SCALE
        live = iota((16, 2048), 1) < lengths[s]
        sc = jnp.where(live, sc, -1e30)
        e = jnp.exp(sc - jnp.max(sc, axis=1, keepdims=True))
        e = jnp.where(live, e, 0.0)
        p = (e / jnp.sum(e, axis=1, keepdims=True)).astype(BF)
        ctxs.append(dot_nt(p, kv[s, 0:512]).astype(BF))
    ctx = jnp.concatenate(ctxs, axis=0)
    wide_c = jnp.concatenate([ctx] * 16, axis=1)
    own_head = iota((32, 8192), 1) // 512 == (iota((32, 8192), 0) & 15)
    wide_c = jnp.where(own_head, wide_c, jnp.zeros_like(wide_c))
    need(l_av)
    heads = dot(wide_c, av[...].reshape(8192, 128)).astype(BF)

    hp = dot(by_dest, heads)
    for zt in range(8):
        hs[zt] = hp[4 * zt : 4 * zt + 4].astype(BF)
    home = x == y
    for kz in FAR_FIRST + (0,):
        zt = (z + kz) % 8
        for kx in (2, 1, 3, 0):
            for kc in (1, 0):
                cp = rcopy(
                    hs.at[zt], hb.at[w], ss_c.at[0], rs_c.at[0],
                    wid(x, zt, (c + kc) % 2), (x + kx) % 4,
                )
                send(cp, x != y if kx == 0 and kz == 0 and kc == 0 else None)
    drain(hb.at[0:63], ss_c.at[0], home)
    drain(hb.at[0:64], ss_c.at[0], jnp.logical_not(home))

    @pl.when(home)
    def _():
        hb[w] = hs[z]
        arrivals(hb.at[0:63], rs_c.at[0])

    @pl.when(jnp.logical_not(home))
    def _():
        arrivals(hb.at[0:64], rs_c.at[0])

    for j in range(64):
        two = hb[j].astype(F32)
        hf[0, 2 * j : 2 * j + 2] = two[0:2]
        hf[1, 2 * j : 2 * j + 2] = two[2:4]
    need(l_wo)
    arrivals(wo.at[128:256], rs_w.at[1])
    both = jnp.concatenate([hf[c], hf[1 - c]], axis=1).astype(BF)
    heads_all = dot(pm[...], both).astype(BF)

    for g, (a, b) in enumerate(GROUPS):
        cols = slice(128 * a, 128 * b)
        part = dot(heads_all, wo[:, cols]).reshape(4, 32, -1)
        pown[:, :, cols] = part
        d1b[:, :, cols] = part.astype(BF)
        for k in (2, 1, 3):
            yt = (y + k) % 4
            send(rcopy(
                d1b.at[yt, :, cols], d1r.at[k - 1, :, cols], ss_d.at[0], rs_d.at[g],
                wid(yt, z, c), x,
            ))
    drain(d1b.at[0:3], ss_d.at[0])
    for g, (a, b) in enumerate(GROUPS):
        cols = slice(128 * a, 128 * b)
        total = pown[y, :, cols] + resmask[:, cols]
        arrivals(d1r.at[:, :, cols], rs_d.at[g])
        for k in range(3):
            total = total + d1r[k, :, cols].astype(F32)
        for j in range(a, b):
            piece = total[:, 128 * (j - a) : 128 * (j - a) + 128]
            asum[j] = piece
            d2b[j] = piece.astype(BF)
            k = (j + 8 - z) % 8
            send(rcopy(d2b.at[j], d2r.at[k], ss_z.at[0], rs_z.at[0], wid(y, j, c), x), z != j)
    drain(d2b.at[0:6], ss_z.at[0], z < 7)
    drain(d2b.at[0:7], ss_z.at[0], z == 7)

    zc = lax.min(z, 6)

    @pl.when(z < 7)
    def _():
        mid = asum[zc]
        arrivals(d2r.at[1:8], rs_z.at[0])
        for k in range(1, 8):
            mid = mid + d2r[k].astype(F32)
        f1[zc] = (mid * gains[zc]).astype(BF)

    zg = sum(jnp.where(zc >= b, 1, 0) for _, b in GROUPS[:-1])
    for k in FAR_FIRST:
        zt = (z + k) % 8
        send(rcopy(f1.at[zc], f1.at[zc], ss_f1.at[0], rs_f1.at[zg], wid(y, zt, c), x), z < 7)
    drain(f1.at[0:7], ss_f1.at[0], z < 7)

    sums = jnp.zeros((32, 1), F32)
    for g, (a, b) in enumerate(GROUPS):
        mine = jnp.logical_and(z >= a, z < b)

        @pl.when(jnp.logical_not(mine))
        def _():
            arrivals(f1.at[a:b], rs_f1.at[g])

        if b - a > 1:
            @pl.when(mine)
            def _():
                arrivals(f1.at[a : b - 1], rs_f1.at[g])

        cols = slice(128 * a, 128 * b)
        x16 = jnp.concatenate([f1[j] for j in range(a, b)], axis=1)
        f2[y, :, cols] = x16
        plain = x16.astype(F32) * inv_own[:, cols]
        sums = sums + jnp.sum(plain * plain, axis=1, keepdims=True)
        if g == NG - 1:
            high = sums.astype(BF).astype(F32)
            tag = jnp.where(iota((32, 128), 1) < 64, high, sums - high)
            f2[y, :, HALF : HALF + 128] = tag.astype(BF)
            cols = slice(128 * a, HALF + 128)
        for k in (2, 1, 3):
            yt = (y + k) % 4
            send(rcopy(
                f2.at[y, :, cols], f2.at[y, :, cols], ss_f2.at[0], rs_f2.at[g], wid(yt, z, c), x
            ))
        send(rcopy(
            f2.at[y, :, cols], f3.at[y, :, cols], ss_f2.at[1], rs_f3.at[g], wid(y, z, 1 - c), x
        ))
    drain(f2.at[0:3], ss_f2.at[0])
    drain(f2.at[0:4], ss_f2.at[1])

    need(l_wga)
    need(l_wua)

    def gate_up(acc, rows, w_gate, w_up, g):
        cols = slice(128 * GROUPS[g][0], 128 * GROUPS[g][1])
        act = rows[:, :, cols].reshape(128, -1)
        new = [dot_nt(act, w_gate[:, cols]), dot_nt(act, w_up[:, cols])]
        return new if acc is None else [p + q for p, q in zip(acc, new)]

    def span(g):
        a, b = GROUPS[g]
        return slice(128 * a, HALF + 128 if g == NG - 1 else 128 * b)

    acc = None
    for g in range(NG):
        arrivals(f2.at[0:3, :, span(g)], rs_f2.at[g])
        for k in (2, 1, 3):
            yb = (y + 4 - k) % 4
            send(rcopy(
                f2.at[yb, :, span(g)], f3.at[yb, :, span(g)], ss_f2.at[1], rs_f3.at[g],
                wid(y, z, 1 - c), x,
            ))
        acc = gate_up(acc, f2, wga, wua, g)
    need(l_wgb)
    need(l_wub)
    for g in range(NG):
        arrivals(f3.at[:, :, span(g)], rs_f3.at[g])
        acc = gate_up(acc, f3, wgb, wub, g)
    tags = f2[:, :, HALF:].reshape(128, 128).astype(F32) + f3[:, :, HALF:].reshape(128, 128).astype(F32)
    sums = tags[:, 0:1] + tags[:, 64:65]
    high = sums.astype(BF).astype(F32)
    tag = jnp.where(iota((128, 128), 1) < 64, high, sums - high).astype(BF)
    gate, up = acc[0].astype(BF), acc[1].astype(BF)
    for b in range(4):
        part = slice(32 * b, 32 * b + 32)
        g1b[b, :, 256:384] = tag[part]
        g1b[b, :, 640:768] = tag[part]
        g1b[b, :, 0:288] = gate[part]
        g1b[b, :, 384:672] = up[part]
    for k in (2, 1, 3):
        xt = (x + k) % 4
        send(rcopy(g1b.at[xt], g1r.at[k], ss_g.at[0], rs_g.at[0], w, xt))

    pick = jnp.where(iota((16, 32), 1) == c * 16 + z * 2 + iota((16, 32), 0), 1.0, 0.0).astype(BF)
    here = dot(pick, f2[y, :, 0:HALF])[0:2] * inv_own[...]
    there = dot(pick, f3[y, :, 0:HALF])[0:2] * inv_other[...]
    mrow[:, 0:HALF] = jnp.where(c == 0, here, there)
    mrow[:, HALF:COLS] = jnp.where(c == 0, there, here)
    drain(g1b.at[0:3], ss_g.at[0])
    total = g1b[x].astype(F32)
    arrivals(g1r.at[1:4], rs_g.at[0])
    for k in range(1, 4):
        total = total + g1r[k].astype(F32)
    square = total[:, 288:289] + total[:, 320:321]
    norm = lax.rsqrt(square / D + 1e-06)
    gate = total[:, 0:288] * norm
    up = total[:, 384:672] * norm
    hid[x] = (gate / (1.0 + jnp.exp(-gate)) * up).astype(BF)
    for k in (2, 1, 3):
        send(rcopy(hid.at[x], hid.at[x], ss_g.at[1], rs_g.at[1], w, (x + k) % 4))
    drain(hid.at[0:3], ss_g.at[1])
    need(l_wd)
    arrivals(hid.at[0:3], rs_g.at[1])

    def to_core(terms, send_buf, recv_buf, own_buf, sems, rsem):
        for g, (a, b) in enumerate(GROUPS):
            cols = slice(256 * a, 256 * b)
            send_buf[:, :, cols] = terms(1, cols).astype(BF).reshape(4, 16, -1)
            send(rcopy(
                send_buf.at[:, :, cols], recv_buf.at[:, :, cols], sems.at[0], rsem.at[g],
                wid(y, z, 1 - c), x,
            ))
        drain(send_buf.at[0:4], sems.at[0])
        for a, b in GROUPS:
            cols = slice(256 * a, 256 * b)
            own_buf[:, :, cols] = terms(0, cols).reshape(4, 16, -1)

    def along_y(own_buf, recv_core, send_buf, recv_buf, sems, rsem):
        for g, (a, b) in enumerate(GROUPS):
            cols = slice(256 * a, 256 * b)
            arrivals(recv_core.at[:, :, cols], rsem.at[g])
            for yp in range(4):
                total = own_buf[yp, :, cols] + recv_core[yp, :, cols].astype(F32)
                own_buf[yp, :, cols] = total
                send_buf[yp, :, cols] = total.astype(BF)
            for k in (2, 1, 3):
                yt = (y + k) % 4
                send(rcopy(
                    send_buf.at[yt, :, cols], recv_buf.at[k - 1, :, cols], sems.at[1],
                    rsem.at[NG + g], wid(yt, z, c), x,
                ))
        drain(send_buf.at[0:3], sems.at[1])

    def y_total(g, own_buf, recv_buf, rsem):
        cols = slice(256 * GROUPS[g][0], 256 * GROUPS[g][1])
        total = own_buf[y, :, cols]
        arrivals(recv_buf.at[:, :, cols], rsem.at[NG + g])
        for k in range(3):
            total = total + recv_buf[k, :, cols].astype(F32)
        return total

    def hidden_of(core):
        return hid[:, pl.ds(pl.multiple_of(core * 16, 16), 16), :].reshape(64, 288)

    hidden = [hidden_of(c), hidden_of(1 - c)]
    to_core(lambda n, cols: dot(hidden[n], wd[:, cols]), h0b, h0r, pown2, ss_h, rs_h)
    along_y(pown2, h0r, h1b, h1r, ss_h, rs_h)
    for g, (a, b) in enumerate(GROUPS):
        cols = slice(256 * a, 256 * b)
        total = y_total(g, pown2, h1r, rs_h)
        for zp in range(8):
            piece = total[2 * zp : 2 * zp + 2]
            h2f[zp, :, cols] = piece
            h2b[zp, :, cols] = piece.astype(BF)
        for k in FAR_FIRST:
            zt = (z + k) % 8
            send(rcopy(
                h2b.at[zt, :, cols], h2r.at[k - 1, :, cols], ss_o.at[0], rs_o.at[g],
                wid(y, zt, c), x,
            ))
    drain(h2b.at[0:7], ss_o.at[0])
    for g, (a, b) in enumerate(GROUPS):
        cols = slice(256 * a, 256 * b)
        total = mrow[:, cols] + h2f[z, :, cols]
        arrivals(h2r.at[:, :, cols], rs_o.at[g])
        for k in range(7):
            total = total + h2r[k, :, cols].astype(F32)
        out[:, cols] = total.astype(BF)

    finish()


def shards(
    residual_in, query_nope, query_rope, absorb_key, absorb_value, latent_cache, cache_lengths,
    slot_rows, out_proj, norm_gain, gate_weight, up_weight, down_weight,
):
    v = pltpu.VMEM
    sem = pltpu.SemaphoreType.DMA
    scratch = [
        v((1, 128), jnp.int32), v((COLS,), BF), v((2, COLS), BF), v((2, 16, 64), BF),
        v((16, 128, 512), BF), v((16, 512, 128), BF), v((2, 576, 2048), BF), v((256, HALF), BF),
        v((288, HALF), BF), v((288, HALF), BF), v((288, HALF), BF), v((288, HALF), BF),
        v((288, COLS), BF), sem((14,)),
        pltpu.SemaphoreType.REGULAR((3,)),
        v((8, 3, 16, 128), BF), v((8, 3, 16, 128), BF), v((8, 3, 16, 128), BF), sem((2,)), sem((2,)),
        v((8, 4, 128), BF), v((64, 4, 128), BF), v((2, 128, 128), F32), sem((1,)), sem((1,)),
        v((128, 128), BF), v((7, 1, 128), F32), v((1, HALF), F32), v((1, HALF), F32),
        v((2, HALF), BF), v((32, HALF), F32), sem((2,)), sem((2,)),
        v((4, 32, HALF), F32), v((4, 32, HALF), BF), v((3, 32, HALF), BF), sem((1,)), sem((NG,)),
        v((7, 32, 128), F32), v((7, 32, 128), BF), v((8, 32, 128), BF), sem((1,)), sem((1,)),
        v((7, 32, 128), BF), v((4, 32, HALF + 128), BF), v((4, 32, HALF + 128), BF),
        v((2, COLS), F32), sem((1,)), sem((NG,)), sem((2,)), sem((NG,)), sem((NG,)),
        v((4, 32, 768), BF), v((4, 32, 768), BF), v((4, 32, 288), BF), sem((2,)), sem((2,)),
        v((4, 16, COLS), BF), v((4, 16, COLS), BF), v((4, 16, COLS), F32), v((4, 16, COLS), BF),
        v((3, 16, COLS), BF), sem((2,)), sem((2 * NG,)),
        v((8, 2, COLS), BF), v((8, 2, COLS), F32), v((7, 2, COLS), BF), sem((1,)), sem((NG,)),
    ]
    return pl.pallas_call(
        kernel,
        out_shape=jax.ShapeDtypeStruct((2, COLS), BF),
        in_specs=[SMEM, SMEM] + [HBM] * 12,
        out_specs=VM,
        scratch_shapes=scratch,
        compiler_params=pltpu.CompilerParams(
            collective_id=0, has_side_effects=True, vmem_limit_bytes=67043328
        ),
    )(
        slot_rows, cache_lengths, slot_rows.reshape(1, 128), norm_gain,
        residual_in, query_nope, query_rope, absorb_key, absorb_value,
        jnp.swapaxes(latent_cache, 1, 2), out_proj, gate_weight.T, up_weight.T, down_weight,
    )


def solution(mesh):
    in_specs = (
        P("wide", "narrow"),
        P("wide", "narrow", None),
        P("wide", "narrow", None),
        P("narrow", None, None),
        P("narrow", None, None),
        P("wide", None, None),
        P("wide"),
        P(),
        P("wide", "narrow"),
        P("narrow"),
        P("narrow", "wide"),
        P("narrow", "wide"),
        P("wide", "narrow"),
    )
    out_specs = P("wide", "narrow")
    return jax.shard_map(shards, mesh=mesh, in_specs=in_specs, out_specs=out_specs, check_vma=False)
```

time: 71.4 us -> 69.9 us (0.979)
  Pallas kernels: 69.9 us -> 68.5 us
    pallas_call x1, Pallas kernels: 69.9 us -> 68.5 us  [shards(): pl.pallas_call(kernel, out_shape=jax.ShapeDtypeStruct((2, COLS), BF), in_...]
where the time goes in v4:
time: 69.9 us; the launch traced here: 69.8 us
  Pallas kernels  68.5 us (98%)
  local copies, waits for them, and re-layouts  1.29 us (2%)
    pallas_call x1, Pallas kernels, shards(): pl.pallas_call(kernel, out_shape=jax.ShapeDtypeStruct((2, COLS), BF), in_...  68.5 us

profile of v4, /device:TPU:1, one launch (start us, length us, event | category | flops | bytes accessed | tf_op | source)
XLA Modules:
  0.0 69.8 jit_solution(925503598698390815)
XLA Ops:
  0.0 68.5 %shard_map.127 = bf16[2,1792]{1,0:T(2,128)(2,1)} custom-call(s32[128]{0:T(128)} %slots.1, s32[2]{0:T(128)} %lengths.1, s32[1,128]{1,0:T(1,128)} %bitcast.7, bf16[1792]{0:T(1024)(128)(2,1)} %gain_h.1, bf16[2,1792]{1,0:T(2,128)(2,1)} %res_h.1, bf16[2,16,128]{2,1,0:T(8,128)(2,1)} %qn_h.1, bf16[2,16,64]{2,1,0:T(8,128)(2,1)} %qr_h.1, bf16[16,128,512]{2,1,0:T(8,128)(2,1)} %ak_h.1, ...), custom_call_target="tpu_custom_call" | custom-call | tf_op jit(solution)/shard_map/pallas_call | solution.py:505
  68.5 1.3 %copy.15 = bf16[2,1792]{1,0:T(2,128)(2,1)} copy(bf16[2,1792]{1,0:T(2,128)(2,1)} %shard_map.127) | data formatting | bytes 14336

commit v5 on v4

--- a/solution.py
+++ b/solution.py
@@ -13,12 +13,12 @@
 BF = jnp.bfloat16
 COLS = 1792
 HALF = COLS // 2
-GROUPS = ((0, 1), (1, 3), (3, 5), (5, 7))
+GROUPS = ((0, 2), (2, 4), (4, 6), (6, 7))
 NG = len(GROUPS)
+LAST = ((0, 1), (2, 3))
 FAR_FIRST = (4, 3, 5, 2, 6, 1, 7)
 SCALE = 1.0 / math.sqrt(192)
 HBM = pl.BlockSpec(memory_space=pltpu.HBM)
-SMEM = pl.BlockSpec(memory_space=pltpu.SMEM)
 VM = pl.BlockSpec(memory_space=pltpu.VMEM)
 
 
@@ -39,16 +39,16 @@
 
 
 def kernel(
-    slots, lengths, slot_vec_h, gain_h,
+    slots_h, lengths_h, slot_vec_h, gain_h,
     res_h, qn_h, qr_h, ak_h, av_h, kv_h, wo_h, wg_h, wu_h, wd_h,
     out,
-    slot_vec, gain_v, res, qr, ak, av, kv, wo, wga, wgb, wua, wub, wd, lsem,
+    slots, lengths, slot_vec, gain_v, res, qr, ak, av, kv, wo, wga, wgb, wua, wub, wd, lsem,
     relay, gq, sq, rq, ss_a, rs_a, hs, hb, hf, ss_c, rs_c,
     pm, gains, inv_own, inv_other, resx, resmask, ss_w, rs_w,
     pown, d1b, d1r, ss_d, rs_d, asum, d2b, d2r, ss_z, rs_z,
     f1, f2, f3, mrow, ss_f1, rs_f1, ss_f2, rs_f2, rs_f3,
     g1b, g1r, hid, ss_g, rs_g,
-    h0b, h0r, pown2, h1b, h1r, ss_h, rs_h, h2b, h2f, h2r, ss_o, rs_o,
+    pown2, h1b, h1r, ss_h, rs_h, h2b, h2f, h2r, ss_o, rs_o,
 ):
     w = lax.axis_index("wide")
     x = lax.axis_index("narrow")
@@ -111,13 +111,15 @@
     def greet(w_, x_):
         pl.semaphore_signal(bar, inc=1, device_id=(w_, x_), device_id_type=MESH)
 
-    for k in range(1, 8):
+    for k in (2, 1, 3):
+        greet(w, (x + k) % 4)
+    for k in (4, 5, 2, 3, 6, 7, 1):
         t = (yc + k) % 8
         greet(wid(t // 2, z, t % 2), x)
     for k in (1, 7):
         greet(wid(y, (z + k) % 8, c), x)
-    for k in range(1, 4):
-        greet(w, (x + k) % 4)
+    l_slots = load(slots_h, slots)
+    l_lengths = load(lengths_h, lengths)
     l_qn = load(qn_h, gq.at[yc, pl.ds(0, 2)])
     l_qr = load(qr_h, qr)
     l_ak = load(ak_h, ak)
@@ -131,7 +133,7 @@
     l_wua = load(wu_h.at[:, own_cols], wua)
     l_wgb = load(wg_h.at[:, other_cols], wgb)
     l_wub = load(wu_h.at[:, other_cols], wub)
-    l_wd = load(wd_h, wd)
+    l_wd = load(wd_h.at[:, own_cols], wd.at[0:288])
 
     pl.semaphore_wait(bar, 12)
     need(l_qr)
@@ -180,20 +182,24 @@
     arrivals(gq.at[0:7], rs_a.at[0])
 
     low = iota((16, 128), 1) < 64
-    for zp in range(8):
+    need(l_slots)
+    need(l_lengths)
+    for kz in FAR_FIRST + (0,):
+        zt = (z + kz) % 8
         ropes = []
         for s in range(2):
-            r = slots[wid(y, zp, c) * 2 + s]
+            r = slots[wid(y, zt, c) * 2 + s]
             i8 = (r // 32) * 2 + ((r // 2) & 1)
             i = r & 1
-            sq[zp, s] = gq[i8, i]
+            sq[zt, s] = gq[i8, i]
             tile = gq[i8, 2].astype(F32)
             ropes.append(jnp.where(i == s, tile, swap_halves(tile)))
-        sq[zp, 2] = jnp.where(low, ropes[0], ropes[1]).astype(BF)
-    for k in FAR_FIRST:
-        zt = (z + k) % 8
-        send(rcopy(sq.at[zt], rq.at[z], ss_a.at[1], rs_a.at[1], wid(y, zt, c), x))
+        sq[zt, 2] = jnp.where(low, ropes[0], ropes[1]).astype(BF)
+        if kz:
+            send(rcopy(sq.at[zt], rq.at[z], ss_a.at[1], rs_a.at[1], wid(y, zt, c), x))
     drain(sq.at[0:7], ss_a.at[1])
+    send(rcopy(wd_h.at[:, other_cols], wd.at[288:576], ss_w.at[2], rs_w.at[2], partner, x))
+    drain(wd.at[288:576], ss_w.at[2])
     rq[z] = sq[z]
     arrivals(resx, rs_w.at[0])
     mine = jnp.where(c == 0, res[:, :HALF], res[:, HALF:]).astype(F32)
@@ -391,8 +397,8 @@
     pick = jnp.where(iota((16, 32), 1) == c * 16 + z * 2 + iota((16, 32), 0), 1.0, 0.0).astype(BF)
     here = dot(pick, f2[y, :, 0:HALF])[0:2] * inv_own[...]
     there = dot(pick, f3[y, :, 0:HALF])[0:2] * inv_other[...]
-    mrow[:, 0:HALF] = jnp.where(c == 0, here, there)
-    mrow[:, HALF:COLS] = jnp.where(c == 0, there, here)
+    mrow[0] = here
+    mrow[1] = there
     drain(g1b.at[0:3], ss_g.at[0])
     total = g1b[x].astype(F32)
     arrivals(g1r.at[1:4], rs_g.at[0])
@@ -402,77 +408,69 @@
     norm = lax.rsqrt(square / D + 1e-06)
     gate = total[:, 0:288] * norm
     up = total[:, 384:672] * norm
-    hid[x] = (gate / (1.0 + jnp.exp(-gate)) * up).astype(BF)
+    hid[0, x] = (gate / (1.0 + jnp.exp(-gate)) * up).astype(BF)
     for k in (2, 1, 3):
-        send(rcopy(hid.at[x], hid.at[x], ss_g.at[1], rs_g.at[1], w, (x + k) % 4))
-    drain(hid.at[0:3], ss_g.at[1])
+        xt = (x + k) % 4
+        send(rcopy(hid.at[0, x], hid.at[1, x], ss_g.at[2], rs_g.at[2], partner, xt))
+        send(rcopy(hid.at[0, x], hid.at[0, x], ss_g.at[1], rs_g.at[1], w, xt))
+    send(rcopy(hid.at[0, x], hid.at[1, x], ss_g.at[2], rs_g.at[2], partner, x))
+    drain(hid.at[0, 0:3], ss_g.at[1])
+    drain(hid.at[1, 0:4], ss_g.at[2])
     need(l_wd)
-    arrivals(hid.at[0:3], rs_g.at[1])
-
-    def to_core(terms, send_buf, recv_buf, own_buf, sems, rsem):
-        for g, (a, b) in enumerate(GROUPS):
-            cols = slice(256 * a, 256 * b)
-            send_buf[:, :, cols] = terms(1, cols).astype(BF).reshape(4, 16, -1)
+    arrivals(wd.at[288:576], rs_w.at[2])
+    arrivals(hid.at[0, 0:3], rs_g.at[1])
+    arrivals(hid.at[1, 0:4], rs_g.at[2])
+
+    near = hid[0].reshape(128, 288)
+    far = hid[1].reshape(128, 288)
+    for g, (a, b) in enumerate(GROUPS):
+        cols = slice(128 * a, 128 * b)
+        part = (dot(near, wd[0:288, cols]) + dot(far, wd[288:576, cols])).reshape(4, 32, -1)
+        pown2[:, :, cols] = part
+        h1b[:, :, cols] = part.astype(BF)
+        for k in (2, 1, 3):
+            yt = (y + k) % 4
             send(rcopy(
-                send_buf.at[:, :, cols], recv_buf.at[:, :, cols], sems.at[0], rsem.at[g],
-                wid(y, z, 1 - c), x,
+                h1b.at[yt, :, cols], h1r.at[k - 1, :, cols], ss_h.at[0], rs_h.at[g],
+                wid(yt, z, c), x,
             ))
-        drain(send_buf.at[0:4], sems.at[0])
-        for a, b in GROUPS:
-            cols = slice(256 * a, 256 * b)
-            own_buf[:, :, cols] = terms(0, cols).reshape(4, 16, -1)
-
-    def along_y(own_buf, recv_core, send_buf, recv_buf, sems, rsem):
-        for g, (a, b) in enumerate(GROUPS):
-            cols = slice(256 * a, 256 * b)
-            arrivals(recv_core.at[:, :, cols], rsem.at[g])
-            for yp in range(4):
-                total = own_buf[yp, :, cols] + recv_core[yp, :, cols].astype(F32)
-                own_buf[yp, :, cols] = total
-                send_buf[yp, :, cols] = total.astype(BF)
-            for k in (2, 1, 3):
-                yt = (y + k) % 4
-                send(rcopy(
-                    send_buf.at[yt, :, cols], recv_buf.at[k - 1, :, cols], sems.at[1],
-                    rsem.at[NG + g], wid(yt, z, c), x,
-                ))
-        drain(send_buf.at[0:3], sems.at[1])
-
-    def y_total(g, own_buf, recv_buf, rsem):
-        cols = slice(256 * GROUPS[g][0], 256 * GROUPS[g][1])
-        total = own_buf[y, :, cols]
-        arrivals(recv_buf.at[:, :, cols], rsem.at[NG + g])
+    drain(h1b.at[0:3], ss_h.at[0])
+    for g, (a, b) in enumerate(GROUPS):
+        cols = slice(128 * a, 128 * b)
+        total = pown2[y, :, cols]
+        arrivals(h1r.at[:, :, cols], rs_h.at[g])
         for k in range(3):
-            total = total + recv_buf[k, :, cols].astype(F32)
-        return total
-
-    def hidden_of(core):
-        return hid[:, pl.ds(pl.multiple_of(core * 16, 16), 16), :].reshape(64, 288)
-
-    hidden = [hidden_of(c), hidden_of(1 - c)]
-    to_core(lambda n, cols: dot(hidden[n], wd[:, cols]), h0b, h0r, pown2, ss_h, rs_h)
-    along_y(pown2, h0r, h1b, h1r, ss_h, rs_h)
-    for g, (a, b) in enumerate(GROUPS):
-        cols = slice(256 * a, 256 * b)
-        total = y_total(g, pown2, h1r, rs_h)
-        for zp in range(8):
-            piece = total[2 * zp : 2 * zp + 2]
-            h2f[zp, :, cols] = piece
-            h2b[zp, :, cols] = piece.astype(BF)
-        for k in FAR_FIRST:
-            zt = (z + k) % 8
-            send(rcopy(
-                h2b.at[zt, :, cols], h2r.at[k - 1, :, cols], ss_o.at[0], rs_o.at[g],
-                wid(y, zt, c), x,
-            ))
-    drain(h2b.at[0:7], ss_o.at[0])
-    for g, (a, b) in enumerate(GROUPS):
-        cols = slice(256 * a, 256 * b)
-        total = mrow[:, cols] + h2f[z, :, cols]
-        arrivals(h2r.at[:, :, cols], rs_o.at[g])
-        for k in range(7):
-            total = total + h2r[k, :, cols].astype(F32)
-        out[:, cols] = total.astype(BF)
+            total = total + h1r[k, :, cols].astype(F32)
+        for j in range(16):
+            piece = total[2 * j : 2 * j + 2]
+            h2f[j, :, cols] = piece
+            h2b[j, :, cols] = piece.astype(BF)
+        for n, (first, last) in enumerate(LAST):
+            if last != g:
+                continue
+            cols = slice(128 * GROUPS[first][0], 128 * b)
+            for kz in FAR_FIRST + (0,):
+                for kc in (1, 0):
+                    if kz or kc:
+                        zt, ct = (z + kz) % 8, (c + kc) % 2
+                        send(rcopy(
+                            h2b.at[ct * 8 + zt, :, cols], h2r.at[kc * 8 + kz, :, cols],
+                            ss_o.at[0], rs_o.at[n], wid(y, zt, ct), x,
+                        ))
+    drain(h2b.at[0:15], ss_o.at[0])
+    for n, (first, last) in enumerate(LAST):
+        a, b = GROUPS[first][0], GROUPS[last][1]
+        cols = slice(128 * a, 128 * b)
+        mine = mrow[0, :, cols] + h2f[c * 8 + z, :, cols]
+        theirs = mrow[1, :, cols]
+        arrivals(h2r.at[1:16, :, cols], rs_o.at[n])
+        for k in range(8):
+            if k:
+                mine = mine + h2r[k, :, cols].astype(F32)
+            theirs = theirs + h2r[8 + k, :, cols].astype(F32)
+        out[:, cols] = jnp.where(c == 0, mine, theirs).astype(BF)
+        right = slice(HALF + 128 * a, HALF + 128 * b)
+        out[:, right] = jnp.where(c == 0, theirs, mine).astype(BF)
 
     finish()
 
@@ -484,28 +482,28 @@
     v = pltpu.VMEM
     sem = pltpu.SemaphoreType.DMA
     scratch = [
+        pltpu.SMEM((128,), jnp.int32), pltpu.SMEM((2,), jnp.int32),
         v((1, 128), jnp.int32), v((COLS,), BF), v((2, COLS), BF), v((2, 16, 64), BF),
         v((16, 128, 512), BF), v((16, 512, 128), BF), v((2, 576, 2048), BF), v((256, HALF), BF),
         v((288, HALF), BF), v((288, HALF), BF), v((288, HALF), BF), v((288, HALF), BF),
-        v((288, COLS), BF), sem((14,)),
+        v((576, HALF), BF), sem((16,)),
         pltpu.SemaphoreType.REGULAR((3,)),
         v((8, 3, 16, 128), BF), v((8, 3, 16, 128), BF), v((8, 3, 16, 128), BF), sem((2,)), sem((2,)),
         v((8, 4, 128), BF), v((64, 4, 128), BF), v((2, 128, 128), F32), sem((1,)), sem((1,)),
         v((128, 128), BF), v((7, 1, 128), F32), v((1, HALF), F32), v((1, HALF), F32),
-        v((2, HALF), BF), v((32, HALF), F32), sem((2,)), sem((2,)),
+        v((2, HALF), BF), v((32, HALF), F32), sem((3,)), sem((3,)),
         v((4, 32, HALF), F32), v((4, 32, HALF), BF), v((3, 32, HALF), BF), sem((1,)), sem((NG,)),
         v((7, 32, 128), F32), v((7, 32, 128), BF), v((8, 32, 128), BF), sem((1,)), sem((1,)),
         v((7, 32, 128), BF), v((4, 32, HALF + 128), BF), v((4, 32, HALF + 128), BF),
-        v((2, COLS), F32), sem((1,)), sem((NG,)), sem((2,)), sem((NG,)), sem((NG,)),
-        v((4, 32, 768), BF), v((4, 32, 768), BF), v((4, 32, 288), BF), sem((2,)), sem((2,)),
-        v((4, 16, COLS), BF), v((4, 16, COLS), BF), v((4, 16, COLS), F32), v((4, 16, COLS), BF),
-        v((3, 16, COLS), BF), sem((2,)), sem((2 * NG,)),
-        v((8, 2, COLS), BF), v((8, 2, COLS), F32), v((7, 2, COLS), BF), sem((1,)), sem((NG,)),
+        v((2, 2, HALF), F32), sem((1,)), sem((NG,)), sem((2,)), sem((NG,)), sem((NG,)),
+        v((4, 32, 768), BF), v((4, 32, 768), BF), v((2, 4, 32, 288), BF), sem((3,)), sem((3,)),
+        v((4, 32, HALF), F32), v((4, 32, HALF), BF), v((3, 32, HALF), BF), sem((1,)), sem((NG,)),
+        v((16, 2, HALF), BF), v((16, 2, HALF), F32), v((16, 2, HALF), BF), sem((1,)), sem((len(LAST),)),
     ]
     return pl.pallas_call(
         kernel,
         out_shape=jax.ShapeDtypeStruct((2, COLS), BF),
-        in_specs=[SMEM, SMEM] + [HBM] * 12,
+        in_specs=[HBM] * 14,
         out_specs=VM,
         scratch_shapes=scratch,
         compiler_params=pltpu.CompilerParams(

time: 69.9 us -> 68.9 us (0.986)
  Pallas kernels: 68.5 us -> 67.4 us
    pallas_call x1, Pallas kernels: 68.5 us -> 67.4 us  [shards(): pl.pallas_call(kernel, out_shape=jax.ShapeDtypeStruct((2, COLS), BF), in_...]
where the time goes in v5:
time: 68.9 us; the launch traced here: 68.7 us
  Pallas kernels  67.4 us (98%)
  local copies, waits for them, and re-layouts  1.29 us (2%)
    pallas_call x1, Pallas kernels, shards(): pl.pallas_call(kernel, out_shape=jax.ShapeDtypeStruct((2, COLS), BF), in_...  67.4 us

profile of v5, /device:TPU:1, one launch (start us, length us, event | category | flops | bytes accessed | tf_op | source)
XLA Modules:
  0.0 68.7 jit_solution(15032742531804246526)
XLA Ops:
  0.0 67.4 %shard_map.127 = bf16[2,1792]{1,0:T(2,128)(2,1)} custom-call(s32[128]{0:T(128)} %slots_h.1, s32[2]{0:T(128)} %lengths_h.1, s32[1,128]{1,0:T(1,128)} %bitcast.7, bf16[1792]{0:T(1024)(128)(2,1)} %gain_h.1, bf16[2,1792]{1,0:T(2,128)(2,1)} %res_h.1, bf16[2,16,128]{2,1,0:T(8,128)(2,1)} %qn_h.1, bf16[2,16,64]{2,1,0:T(8,128)(2,1)} %qr_h.1, ...), custom_call_target="tpu_custom_call" | custom-call | tf_op jit(solution)/shard_map/pallas_call | solution.py:503
  67.4 1.3 %copy.15 = bf16[2,1792]{1,0:T(2,128)(2,1)} copy(bf16[2,1792]{1,0:T(2,128)(2,1)} %shard_map.127) | data formatting | bytes 14336

commit v6 on v5

--- a/solution.py
+++ b/solution.py
@@ -390,9 +390,8 @@
         g1b[b, :, 640:768] = tag[part]
         g1b[b, :, 0:288] = gate[part]
         g1b[b, :, 384:672] = up[part]
-    for k in (2, 1, 3):
-        xt = (x + k) % 4
-        send(rcopy(g1b.at[xt], g1r.at[k], ss_g.at[0], rs_g.at[0], w, xt))
+        k = (b + 4 - x) % 4
+        send(rcopy(g1b.at[b], g1r.at[k], ss_g.at[0], rs_g.at[0], w, b), x != b)
 
     pick = jnp.where(iota((16, 32), 1) == c * 16 + z * 2 + iota((16, 32), 0), 1.0, 0.0).astype(BF)
     here = dot(pick, f2[y, :, 0:HALF])[0:2] * inv_own[...]

time: 68.9 us -> 69.4 us (level)
  no operation moved by 1% of the time
where the time goes in v6:
time: 69.4 us; the launch traced here: 69.3 us
  Pallas kernels  68 us (98%)
  local copies, waits for them, and re-layouts  1.29 us (2%)
    pallas_call x1, Pallas kernels, shards(): pl.pallas_call(kernel, out_shape=jax.ShapeDtypeStruct((2, COLS), BF), in_...  68 us

profile of v6, /device:TPU:1, one launch (start us, length us, event | category | flops | bytes accessed | tf_op | source)
XLA Modules:
  0.0 69.3 jit_solution(8990455566697218364)
XLA Ops:
  0.0 68.0 %shard_map.127 = bf16[2,1792]{1,0:T(2,128)(2,1)} custom-call(s32[128]{0:T(128)} %slots_h.1, s32[2]{0:T(128)} %lengths_h.1, s32[1,128]{1,0:T(1,128)} %bitcast.7, bf16[1792]{0:T(1024)(128)(2,1)} %gain_h.1, bf16[2,1792]{1,0:T(2,128)(2,1)} %res_h.1, bf16[2,16,128]{2,1,0:T(8,128)(2,1)} %qn_h.1, bf16[2,16,64]{2,1,0:T(8,128)(2,1)} %qr_h.1, ...), custom_call_target="tpu_custom_call" | custom-call | tf_op jit(solution)/shard_map/pallas_call | solution.py:502
  68.0 1.3 %copy.15 = bf16[2,1792]{1,0:T(2,128)(2,1)} copy(bf16[2,1792]{1,0:T(2,128)(2,1)} %shard_map.127) | data formatting | bytes 14336
